TPU v7x, 32 devices: a whole 2x2x4 slice. The times are simulated.
32 devices in a mesh: fsdp: 32 (over z, y, x, core).
Axes of the slice: x: 2, y: 2, z: 4, core: 2. Of those that a mesh axis runs over, the one named last changes fastest.
Arguments:
- hidden: bfloat16 [2, 32, 128, 1024], P(None, 'fsdp'), may hold values from -6 to 6
- encoder: bfloat16 [2, 32, 256, 1024], P(None, 'fsdp'), may hold values from -6 to 6
- cotangent: bfloat16 [2, 32, 128, 1024], P(None, 'fsdp'), may hold values from -6 to 6
- segment_ids: int32 [2, 32, 128], replicated, may hold values from 0 to 3, never falling along the last dimension, each value on 1 to 64 neighbouring positions
- rel_buckets: int32 [2, 32, 128], replicated, may hold values from 0 to 31
- enc_rows: int32 [2, 32], replicated, may hold values from 64 to 256, as said below
- dealing: int32 [2, 32], replicated, may hold values from 0 to 31, each once within a row
- gain_self: bfloat16 [1024], P('fsdp'), may hold values from 0.5 to 1.5
- gain_cross: bfloat16 [1024], P('fsdp'), may hold values from 0.5 to 1.5
- gain_ffn: bfloat16 [1024], P('fsdp'), may hold values from 0.5 to 1.5
- rel_bias: bfloat16 [512], P('fsdp'), may hold values from -4 to 4
- self_query: bfloat16 [1024, 1024], P('fsdp'), may hold values from -0.046875 to 0.046875
- self_key: bfloat16 [1024, 1024], P('fsdp'), may hold values from -0.1875 to 0.1875
- self_value: bfloat16 [1024, 1024], P('fsdp'), may hold values from -0.1875 to 0.1875
- self_out: bfloat16 [1024, 1024], P('fsdp'), may hold values from -0.5 to 0.5
- cross_query: bfloat16 [1024, 1024], P('fsdp'), may hold values from -0.046875 to 0.046875
- cross_key: bfloat16 [1024, 1024], P('fsdp'), may hold values from -0.1875 to 0.1875
- cross_value: bfloat16 [1024, 1024], P('fsdp'), may hold values from -0.1875 to 0.1875
- cross_out: bfloat16 [1024, 1024], P('fsdp'), may hold values from -0.5 to 0.5
- feed_gate: bfloat16 [1024, 2816], P('fsdp'), may hold values from -0.1875 to 0.1875
- feed_up: bfloat16 [1024, 2816], P('fsdp'), may hold values from -0.1875 to 0.1875
- feed_down: bfloat16 [2816, 1024], P('fsdp'), may hold values from -0.15625 to 0.15625
Outputs:
- layer_out: bfloat16 [2, 32, 128, 1024], P(None, 'fsdp')
- grad_hidden: float32 [2, 32, 128, 1024], P(None, 'fsdp')
- grad_encoder: float32 [2, 32, 256, 1024], P(None, 'fsdp')
- grad_gain_self: float32 [1024], P('fsdp')
- grad_gain_cross: float32 [1024], P('fsdp')
- grad_gain_ffn: float32 [1024], P('fsdp')
- grad_rel_bias: float32 [512], P('fsdp')
- grad_self_query: float32 [1024, 1024], P('fsdp')
- grad_self_key: float32 [1024, 1024], P('fsdp')
- grad_self_value: float32 [1024, 1024], P('fsdp')
- grad_self_out: float32 [1024, 1024], P('fsdp')
- grad_cross_query: float32 [1024, 1024], P('fsdp')
- grad_cross_key: float32 [1024, 1024], P('fsdp')
- grad_cross_value: float32 [1024, 1024], P('fsdp')
- grad_cross_out: float32 [1024, 1024], P('fsdp')
- grad_feed_gate: float32 [1024, 2816], P('fsdp')
- grad_feed_up: float32 [1024, 2816], P('fsdp')
- grad_feed_down: float32 [2816, 1024], P('fsdp')
Inputs may be any that keep to these rules, and one draw needn't show every extreme that they name: `enc_rows`: live encoder rows of each block; in every micro-batch some block has all 256. `dealing`: each micro-batch's row names every block once. `segment_ids`: document ids never fall along a block; a document has at most 64 tokens.
All inputs are finite; a program needn't handle non-finite values.
Results may differ from a plain program's by a relative error of at most 0.02.
The roundings to bfloat16 on the way count: a program that leaves them out, or rounds other values in their place, can miss the bound.
Values may be sent and summed in bfloat16 or wider, within the bound.
A program may use at most 192 MiB of HBM per device.

v0:
```python
import functools

import jax
import jax.numpy as jnp
from jax import lax
from jax.experimental import pallas as pl
from jax.experimental.pallas import tpu as pltpu
from jax.sharding import PartitionSpec as P

D = 1024
H = 16
DH = 64
NB = 32

AXIS = "fsdp"
eps_norm = 1e-06
masked_score = -1000000000.0
highest = lax.Precision.HIGHEST
f32 = jnp.float32
bf16 = jnp.bfloat16


def product(left_side, right_side):
    return jnp.dot(left_side, right_side, preferred_element_type=f32)


def product_left(left_side, right_side):
    return lax.dot_general(
        left_side, right_side, (((0,), (0,)), ((), ())), preferred_element_type=f32
    )


def product_right(left_side, right_side):
    return lax.dot_general(
        left_side, right_side, (((1,), (1,)), ((), ())), preferred_element_type=f32
    )


def inverse_rms(values):
    return lax.rsqrt(jnp.mean(values * values, axis=-1, keepdims=True) + eps_norm)


def norm_back(values, inverse, gain_row, grad):
    scaled = values * inverse
    weighted = grad * gain_row
    centre = jnp.mean(weighted * scaled, axis=-1, keepdims=True)
    return inverse * (weighted - scaled * centre), jnp.sum(grad * scaled, axis=0)


def gelu_parts(gate_pre):
    root = 0.7978845608028654
    inner = root * (gate_pre + 0.044715 * gate_pre * gate_pre * gate_pre)
    curve = jnp.tanh(inner)
    value = 0.5 * gate_pre * (1.0 + curve)
    slope = 0.5 * (1.0 + curve) + 0.5 * gate_pre * (1.0 - curve * curve) * root * (
        1.0 + 3 * 0.044715 * gate_pre * gate_pre
    )
    return value, slope


def toeplitz_expand(per_offset):
    head_count, length = per_offset.shape
    filler = jnp.zeros((head_count, 1), f32)
    pattern = jnp.concatenate(
        [per_offset[:, :1], filler, per_offset[:, ::-1][:, : length - 1]], axis=1
    )
    tiled_rows = jnp.broadcast_to(pattern[:, None, :], (head_count, length, length + 1))
    return tiled_rows.reshape(head_count, length * (length + 1))[:, : length * length].reshape(
        head_count, length, length
    )


def toeplitz_fold(score_grid):
    head_count, length = (score_grid.shape[0], score_grid.shape[1])
    flat_grid = score_grid.reshape(head_count, length * length)
    padded = jnp.concatenate([flat_grid, jnp.zeros((head_count, length), f32)], axis=1)
    columns = jnp.sum(padded.reshape(head_count, length, length + 1), axis=1)
    return jnp.concatenate([columns[:, :1], columns[:, 2:][:, ::-1]], axis=1)


def heads(matrix, blocks):
    return matrix.reshape(blocks, -1, H, DH)


def score_block(queries, keys_in, bias_grid, allowed):
    scores = jnp.einsum("bihd,bjhd->bhij", queries, keys_in, preferred_element_type=f32)
    if bias_grid is not None:
        scores = scores + bias_grid
    return jnp.where(allowed[:, None], scores, masked_score)


def attend(queries, keys_in, values, bias_grid, allowed):
    blocks = allowed.shape[0]
    scores = score_block(heads(queries, blocks), heads(keys_in, blocks), bias_grid, allowed)
    largest = jnp.max(scores, axis=3, keepdims=True)
    weights = jnp.exp(scores - largest)
    probs = weights / jnp.sum(weights, axis=3, keepdims=True)
    mixed = jnp.einsum(
        "bhij,bjhd->bihd", probs.astype(bf16), heads(values, blocks), preferred_element_type=f32
    )
    return mixed.reshape(queries.shape[0], D).astype(bf16), probs


def attend_back(queries, keys_in, values, probs, grad_mixed):
    blocks = probs.shape[0]
    grad_heads = heads(grad_mixed, blocks)
    grad_values = jnp.einsum(
        "bhij,bihd->bjhd", probs.astype(bf16), grad_heads, preferred_element_type=f32
    )
    grad_probs = jnp.einsum(
        "bihd,bjhd->bhij", grad_heads, heads(values, blocks), preferred_element_type=f32
    )
    grad_scores = (
        probs * (grad_probs - jnp.sum(probs * grad_probs, axis=3, keepdims=True))
    ).astype(bf16)
    grad_queries = jnp.einsum(
        "bhij,bjhd->bihd", grad_scores, heads(keys_in, blocks), preferred_element_type=f32
    )
    grad_keys = jnp.einsum(
        "bhij,bihd->bjhd", grad_scores, heads(queries, blocks), preferred_element_type=f32
    )
    return (
        grad_queries.reshape(-1, D).astype(bf16),
        grad_keys.reshape(-1, D).astype(bf16),
        grad_values.reshape(-1, D).astype(bf16),
        grad_scores,
    )


def redeal(blocks, source):
    micro, own, rows, width = blocks.shape
    count = source.shape[1] // own
    cut = blocks.reshape(micro, own, count, rows // count, width).transpose(2, 0, 1, 3, 4)
    spread = lax.all_to_all(cut, AXIS, split_axis=0, concat_axis=0, tiled=True)
    spread = spread.transpose(1, 0, 2, 3, 4).reshape(micro, count * own, rows // count, width)
    moved = jnp.take_along_axis(spread, source[:, :, None, None], axis=1)
    moved = moved.reshape(micro, count, own, rows // count, width).transpose(1, 0, 2, 3, 4)
    home = lax.all_to_all(moved, AXIS, split_axis=0, concat_axis=0, tiled=True)
    return home.transpose(1, 2, 0, 3, 4).reshape(micro, own, rows, width)


def gather_weights(wide, deep):
    packed = lax.all_gather(jnp.concatenate(wide, axis=1), AXIS, axis=0, tiled=True)
    whole, start = [], 0
    for part in wide:
        whole.append(packed[:, start : start + part.shape[1]])
        start += part.shape[1]
    return whole, lax.all_gather(deep, AXIS, axis=0, tiled=True)


def scatter_grads(wide, deep):
    packed = jnp.concatenate([part.astype(bf16) for part in wide], axis=1)
    packed = lax.psum_scatter(packed, AXIS, scatter_dimension=0, tiled=True).astype(f32)
    pieces, start = [], 0
    for part in wide:
        pieces.append(packed[:, start : start + part.shape[1]])
        start += part.shape[1]
    deep = lax.psum_scatter(deep.astype(bf16), AXIS, scatter_dimension=0, tiled=True)
    return pieces, deep.astype(f32)


MESH = pl.DeviceIdType.MESH
RING = 3
SLOTS = 5


class Place:
    def __init__(self, depth):
        self.depth = depth
        self.count = depth * 8
        self.me = lax.axis_index(AXIS)
        self.core = self.me % 2
        self.x = (self.me // 2) % 2
        self.y = (self.me // 4) % 2
        self.z = self.me // 8
        self.twin = self.me + 1 - 2 * self.core
        self.over_x = self.me + 2 - 4 * self.x
        self.over_y = self.me + 4 - 8 * self.y
        self.far = [(self.z + d) % depth for d in range(1, depth)]
        self.over_z = [self.me + (z - self.z) * 8 for z in self.far]

    def greet(self):
        barrier = pltpu.get_barrier_semaphore()

        def hello(d, _):
            peer = (self.me + d) % self.count
            pl.semaphore_signal(barrier, inc=1, device_id=(peer,), device_id_type=MESH)
            return 0

        lax.fori_loop(1, self.count, hello, 0)
        pl.semaphore_wait(barrier, self.count - 1)


def remote(source, target, send, recv, index, device):
    return pltpu.make_async_remote_copy(
        src_ref=source,
        dst_ref=target,
        send_sem=send.at[index],
        recv_sem=recv.at[index],
        device_id=(device,),
        device_id_type=MESH,
    )


def columns(start, width):
    return pl.ds(pl.multiple_of(start, 128), width)


class Gather:
    def __init__(self, place, pieces, staged, wholes, local, send, recv):
        self.place, self.pieces = place, pieces
        self.staged, self.wholes = staged, wholes
        self.local, self.send, self.recv = local, send, recv
        self.steps = 1 + 2 * (place.depth + 2)
        self.sent = []

    def begin(self, copy):
        copy.start()
        self.sent.append(copy)

    def rows(self, kind):
        height = self.staged[kind].shape[0]
        p = self.place
        return self.wholes[kind].at[p.z, p.y, p.x, pl.ds(p.core * height, height)]

    def quarter(self, i, core, order):
        kind, start, width = self.pieces[i]
        return columns(start + core * (width // 2) + order * (width // 4), width // 4)

    def copy(self, source, target, i, step, device):
        return remote(source, target, self.send, self.recv, i * self.steps + step, device)

    def to_twin(self, i):
        kind, start, width = self.pieces[i]
        cols = columns(start + (1 - self.place.core) * (width // 2), width // 2)
        return self.copy(
            self.staged[kind].at[:, cols], self.rows(kind).at[:, cols], i, 0, self.place.twin
        )

    def own(self, i):
        kind, start, width = self.pieces[i]
        cols = columns(start + self.place.core * (width // 2), width // 2)
        return pltpu.make_async_copy(
            self.staged[kind].at[:, cols], self.rows(kind).at[:, cols], self.local.at[i]
        )

    def along_z(self, i, order, d):
        p = self.place
        ref = self.wholes[self.pieces[i][0]].at[p.z, p.y, p.x, :, self.quarter(i, p.core, order)]
        return self.copy(ref, ref, i, 1 + order * (p.depth + 2) + d, p.over_z[d])

    def plane(self, i, order, second):
        p = self.place
        whole = self.wholes[self.pieces[i][0]]
        cols = self.quarter(i, p.core, order)
        if second:
            ref = whole.at[:, :, p.x, :, cols] if order else whole.at[:, p.y, :, :, cols]
        else:
            ref = whole.at[:, p.y, p.x, :, cols]
        device = p.over_x if order == second else p.over_y
        return self.copy(ref, ref, i, 1 + order * (p.depth + 2) + p.depth - 1 + second, device)

    def across(self, i, order):
        p = self.place
        whole = self.wholes[self.pieces[i][0]]
        ref = whole.at[:, :, :, :, self.quarter(i, p.core, order)]
        return self.copy(ref, ref, i, 1 + order * (p.depth + 2) + p.depth + 1, p.twin)

    def open(self):
        for i in range(len(self.pieces)):
            self.begin(self.to_twin(i))
        for i in range(len(self.pieces)):
            self.own(i).start()
        for i in range(len(self.pieces)):
            self.own(i).wait()
        for i in range(len(self.pieces)):
            self.to_twin(i).wait_recv()
            for d in range(self.place.depth - 1):
                for order in (0, 1):
                    self.begin(self.along_z(i, order, d))

    def advance(self, i, stage):
        if not 0 <= i < len(self.pieces):
            return
        for order in (0, 1):
            if stage == 0:
                for d in range(self.place.depth - 1):
                    self.along_z(i, order, d).wait_recv()
                self.begin(self.plane(i, order, 0))
            elif stage == 1:
                self.plane(i, order, 0).wait_recv()
                self.begin(self.plane(i, order, 1))
            elif stage == 2:
                self.plane(i, order, 1).wait_recv()
                self.begin(self.across(i, order))
            else:
                self.across(i, order).wait_recv()

    def turn(self, t):
        for stage in (3, 2, 1, 0):
            self.advance(t - stage, stage)

    def close(self):
        for copy in self.sent:
            copy.wait_send()


class Scatter:
    def __init__(self, place, pieces, blocks, outs, scratch):
        self.place, self.pieces, self.blocks, self.outs = place, pieces, blocks, outs
        self.grads, self.got, self.final, (self.local, self.send, self.recv) = (
            scratch[0],
            scratch[1:5],
            scratch[5],
            scratch[6:9],
        )
        self.steps = 1 + 2 * (place.depth + 2)
        self.time = 0

    @staticmethod
    def scratch(pieces, depth, blocks):
        tall = max(blocks[kind] * (width // 512) for kind, _, width in pieces)
        copies = len(pieces) * (1 + 2 * (depth + 2))
        return [
            pltpu.VMEM((SLOTS, 2, 2, depth, 2, 2, tall, 128), bf16),
            pltpu.VMEM((RING, 2, depth, 2, 2, tall, 128), bf16),
            pltpu.VMEM((RING, 2, depth, 2, tall, 128), bf16),
            pltpu.VMEM((RING, 2, depth, tall, 128), bf16),
            pltpu.VMEM((RING, 2, depth - 1, tall, 128), bf16),
            pltpu.VMEM((RING, 2, 2, tall // 2, 128), f32),
            pltpu.SemaphoreType.DMA((2 * len(pieces),)),
            pltpu.SemaphoreType.DMA((copies,)),
            pltpu.SemaphoreType.DMA((copies,)),
        ]

    def size(self, i):
        kind, start, width = self.pieces[i]
        return kind, start // 128, width // 512, self.blocks[kind]

    def rows(self, i):
        _, _, tiles, block = self.size(i)
        return pl.ds(0, tiles * block)

    def cut(self, ref, i):
        return ref.at[(slice(None),) * (len(ref.shape) - 2) + (self.rows(i),)]

    def mine(self, i, half, *quarter):
        return self.cut(self.grads.at[(i % SLOTS, half) + quarter], i)

    def theirs(self, level, i, *index):
        return self.cut(self.got[level].at[(i % RING,) + index], i)

    def copy(self, source, target, i, step, device):
        return remote(source, target, self.send, self.recv, i * self.steps + step, device)

    def to_twin(self, i):
        return self.copy(
            self.mine(i, 1 - self.place.core), self.theirs(0, i), i, 0, self.place.twin
        )

    def plane(self, i, order, second):
        p = self.place
        ref = self.mine(i, p.core, order)
        if second:
            ref = ref.at[:, p.y, 1 - p.x] if order else ref.at[:, 1 - p.y, p.x]
        else:
            ref = ref.at[:, 1 - p.y] if order else ref.at[:, :, 1 - p.x]
        device = p.over_x if order == second else p.over_y
        step = 1 + order * (p.depth + 2) + second
        return self.copy(ref, self.theirs(1 + second, i, order), i, step, device)

    def along_z(self, i, order, d):
        p = self.place
        ref = self.mine(i, p.core, order).at[p.far[d], p.y, p.x]
        step = 1 + order * (p.depth + 2) + 2 + d
        return self.copy(ref, self.theirs(3, i, order, d), i, step, p.over_z[d])

    def ends(self, i, order, core):
        kind, first, tiles, block = self.size(i)
        count = tiles * block // 2
        row = (first + (2 * self.place.core + order) * tiles) * (block // 2)
        source = self.final.at[i % RING, order, core, pl.ds(0, count)]
        return source, self.outs[kind].at[pl.ds(pl.multiple_of(row, 8), count)]

    def rest(self, i, order):
        p = self.place
        source, target = self.ends(i, order, 1 - p.core)
        return self.copy(source, target, i, 1 + order * (p.depth + 2) + p.depth + 1, p.twin)

    def keep(self, i, order):
        source, target = self.ends(i, order, self.place.core)
        return pltpu.make_async_copy(source, target, self.local.at[2 * i + order])

    def add(self, i, order, level, spots):
        rows = self.rows(i)
        slot, ring, core = i % SLOTS, i % RING, self.place.core

        def layer(z, _):
            for there, here in spots:
                at = (slot, core, order, z) + here + (rows,)
                total = self.grads[at].astype(f32)
                total = total + self.got[level][(ring, order, z) + there + (rows,)].astype(f32)
                self.grads[at] = total.astype(bf16)
            return 0

        lax.fori_loop(0, self.place.depth, layer, 0)

    def advance(self, i, stage):
        if not 0 <= i < len(self.pieces):
            return
        p = self.place
        if stage == 1:
            self.to_twin(i).wait_recv()
            for order in (0, 1):
                self.add(i, order, 0, [((y, x), (y, x)) for y in (0, 1) for x in (0, 1)])
                self.plane(i, order, 0).start()
        elif stage == 2:
            for order in (0, 1):
                self.plane(i, order, 0).wait_recv()
                self.add(
                    i, order, 1, [((k,), (p.y, k) if order else (k, p.x)) for k in (0, 1)]
                )
                self.plane(i, order, 1).start()
        elif stage == 3:
            for order in (0, 1):
                self.plane(i, order, 1).wait_recv()
                self.add(i, order, 2, [((), (p.y, p.x))])
                for d in range(p.depth - 1):
                    self.along_z(i, order, d).start()
        elif stage == 4:
            if i >= RING:
                self.settle(i - RING)
            _, _, tiles, block = self.size(i)
            rows, half = self.rows(i), block // 2
            for order in (0, 1):
                for d in range(p.depth - 1):
                    self.along_z(i, order, d).wait_recv()
                total = self.grads[i % SLOTS, p.core, order, p.z, p.y, p.x, rows].astype(f32)
                for d in range(p.depth - 1):
                    total = total + self.got[3][i % RING, order, d, rows].astype(f32)
                for tile in range(tiles):
                    for core in (0, 1):
                        row = tile * block + core * half
                        self.final[i % RING, order, core, pl.ds(tile * half, half)] = total[
                            row : row + half
                        ]
                self.rest(i, order).start()
                self.keep(i, order).start()
        else:
            self.to_twin(i).wait_send()
            for order in (0, 1):
                self.plane(i, order, 0).wait_send()
                self.plane(i, order, 1).wait_send()
                for d in range(p.depth - 1):
                    self.along_z(i, order, d).wait_send()
                self.rest(i, order).wait_recv()

    def settle(self, i):
        for order in (0, 1):
            self.rest(i, order).wait_send()
            self.keep(i, order).wait()

    def turn(self):
        for stage in (5, 4, 3, 2, 1):
            self.advance(self.time - stage, stage)
        self.time += 1

    def produce(self, left, right, column):
        i = self.time
        self.turn()
        _, _, tiles, block = self.size(i)
        slot = i % SLOTS
        group = 1 if block % 32 == 0 else 2
        turns = self.place.depth // group
        high = 4 * block * group

        def chunk(k, _):
            n, first = k // turns, (k % turns) * group
            part = transposed(
                left[:, columns(k % turns * high, high)], right[:, columns(column + 256 * n, 256)]
            ).astype(bf16)
            for tile in (0, 1):
                for b in range(4 * group):
                    spot = first + b // 4, b // 2 % 2, b % 2
                    piece = part[b * block : b * block + block, tile * 128 : tile * 128 + 128]
                    if tiles == 2:
                        at = (slot, n // 2, n % 2) + spot + (pl.ds(tile * block, block),)
                    else:
                        at = (slot, n, tile) + spot + (pl.ds(0, block),)
                    self.grads[at] = piece
            return 0

        lax.fori_loop(0, 2 * tiles * turns, chunk, 0)
        self.to_twin(i).start()

    def close(self):
        while self.time < len(self.pieces) + 5:
            self.turn()
        for i in range(max(0, len(self.pieces) - RING), len(self.pieces)):
            self.settle(i)


class Redeal:
    def __init__(self, place, given, spread, moved, wanted, send, recv):
        self.place, self.given, self.spread, self.moved = place, given, spread, moved
        self.wanted, self.send, self.recv = wanted, send, recv
        self.high, self.wide = spread.shape[2:]

    def spot(self, ref, j):
        depth = self.place.depth
        rows = pl.ds(pl.multiple_of((j // depth) * self.high, self.high), self.high)
        return ref.at[:, rows, columns((j % depth) * self.wide, self.wide)]

    def peer(self, d):
        return (self.place.me + d) % self.place.count

    def out(self, d):
        target = self.spread.at[self.place.me]
        peer = self.peer(d)
        return remote(self.spot(self.given, peer), target, self.send, self.recv, d - 1, peer)

    def home(self, d):
        peer, count = self.peer(d), self.place.count
        target = self.spot(self.wanted, self.place.me)
        return remote(
            self.moved.at[peer], target, self.send, self.recv, count - 1 + d - 1, peer
        )

    def each(self, act):
        def one(d, _):
            act(d)
            return 0

        lax.fori_loop(1, self.place.count, one, 0)

    def own(self, ref):
        j = self.place.me
        depth = self.place.depth
        rows = pl.ds(pl.multiple_of((j // depth) * self.high, self.high), self.high)
        return slice(None), rows, columns((j % depth) * self.wide, self.wide)

    def begin(self):
        self.each(lambda d: self.out(d).start())
        self.spread[self.place.me] = self.given[self.own(self.given)]

    def middle(self, source):
        self.each(lambda d: self.out(d).wait())

        def one(j, _):
            for m in range(self.moved.shape[1]):
                self.moved[j, m] = self.spread[source[m, j], m]
            return 0

        lax.fori_loop(0, self.place.count, one, 0)
        self.each(lambda d: self.home(d).start())
        self.wanted[self.own(self.wanted)] = self.moved[self.place.me]

    def end(self):
        self.each(lambda d: self.home(d).wait())


def spread_small(place, tile, table, send, recv):
    table[place.me] = tile[...]

    def out(d, _):
        remote(
            tile, table.at[place.me], send, recv, d - 1, (place.me + d) % place.count
        ).start()
        return 0

    lax.fori_loop(1, place.count, out, 0)


def collect_small(place, tile, table, send, recv):
    def back(d, _):
        copy = remote(
            tile,
            table.at[(place.me + place.count - d) % place.count],
            send,
            recv,
            d - 1,
            (place.me + d) % place.count,
        )
        copy.wait()
        return 0

    lax.fori_loop(1, place.count, back, 0)


def cut_columns(widths, start=0):
    pieces = []
    for width in widths:
        pieces.append((0, start, width))
        start += width
    return pieces


def kernel_depth(count, wide, deep):
    fits = count % 8 == 0 and wide.shape[0] % 8 == 0 and deep.shape[0] % 8 == 0
    return count // 8 if fits else 0


def transposed(left, right):
    return lax.dot_general(
        left, right, (((0,), (0,)), ((), ())), preferred_element_type=f32
    )


def against(left, right):
    return lax.dot_general(
        left, right, (((1,), (1,)), ((), ())), preferred_element_type=f32
    )


class Stream:
    def __init__(self, refs, tiles, slots, sems):
        self.refs, self.tiles, self.slots, self.sems = refs, tiles, slots, sems
        self.next, self.begun = 0, 0

    def copy(self, k):
        kind, start, size = self.tiles[k]
        slot = k % self.slots.shape[0]
        cut = pl.ds(0, size)
        if kind:
            source, target = self.refs[1].at[pl.ds(start, size)], self.slots.at[slot, cut]
        else:
            source, target = self.refs[0].at[:, pl.ds(start, size)], self.slots.at[slot, :, cut]
        return pltpu.make_async_copy(source, target, self.sems.at[slot])

    def take(self):
        ahead = min(len(self.tiles), self.next + self.slots.shape[0])
        while self.begun < ahead:
            self.copy(self.begun).start()
            self.begun += 1
        k = self.next
        self.copy(k).wait()
        self.next += 1
        return self.slots.at[k % self.slots.shape[0]]


def back_into(total, left, start, size, tile, fresh):
    def chunk(n, _):
        cols = columns(n * 256, 256)
        part = against(left[:, start : start + size], tile[cols, 0:size])
        rows = pl.ds(0, left.shape[0])
        total[rows, cols] = part if fresh else total[rows, cols] + part
        return 0

    lax.fori_loop(0, D // 256, chunk, 0)


def back_rounded(out, left, tile):
    def chunk(n, _):
        cols = columns(n * 256, 256)
        out[:, cols] = against(left[...], tile[cols, :]).astype(bf16)
        return 0

    lax.fori_loop(0, D // 256, chunk, 0)


def self_scores(bias, scores, block, head):
    marked = bias[block, head].astype(f32)
    return jnp.where(marked < -1e29, masked_score, scores + marked)


def cross_scores(live, scores, block, head):
    return jnp.where(live[block, 0:1, :] > 0.0, scores, masked_score)


def pair_loop(count, body_of):
    def one(index, _):
        body_of(index // (H // 2), index % (H // 2))
        return 0

    lax.fori_loop(0, count * (H // 2), one, 0)


def softmax_rows(scores):
    weights = jnp.exp(scores - jnp.max(scores, axis=1, keepdims=True))
    return weights / jnp.sum(weights, axis=1, keepdims=True)


def attend_back_pairs(refs, grads, marks, mask, folded):
    q, k, v, da = refs
    dq, dk, dv = grads
    rows_q = 128
    tall = k.shape[0] // (q.shape[0] // rows_q)
    even = lax.broadcasted_iota(jnp.int32, (1, 128), 1) < DH
    down, right = [lax.broadcasted_iota(jnp.int32, (rows_q, rows_q), k) for k in (0, 1)]
    mirror = jnp.where(down + right == rows_q - 1, 1.0, 0.0).astype(bf16)

    def pair(block, p):
        rows = pl.ds(pl.multiple_of(block * rows_q, rows_q), rows_q)
        keys = pl.ds(pl.multiple_of(block * tall, tall), tall)
        cols = columns(p * 128, 128)
        q2, k2, v2, da2 = q[rows, cols], k[keys, cols], v[keys, cols], da[rows, cols]
        sums = [None, None, None]
        for e in (0, 1):
            keep = even if e == 0 else jnp.logical_not(even)

            def half(value):
                return jnp.where(keep, value.astype(f32), 0.0).astype(bf16)

            qe, dae, ke = half(q2), half(da2), half(k2)
            head = 2 * p + e
            probs = softmax_rows(mask(marks, against(qe, k2), block, head))
            dp = against(dae, v2)
            centre = jnp.sum(probs * dp, axis=1, keepdims=True)
            ds = (probs * (dp - centre)).astype(bf16)
            terms = (
                jnp.dot(ds, ke, preferred_element_type=f32),
                transposed(ds, qe),
                transposed(probs.astype(bf16), dae),
            )
            sums = [t if s is None else s + t for s, t in zip(sums, terms)]
            if folded is not None:
                upside = jnp.dot(mirror, ds, preferred_element_type=f32)
                turned = pltpu.roll(upside, 0, 1, stride=1, stride_axis=0)
                folded[block * H + head] = jnp.sum(turned, axis=0, keepdims=True)
        dq[rows, cols] = sums[0].astype(bf16)
        dk[keys, cols] = sums[1].astype(bf16)
        dv[keys, cols] = sums[2].astype(bf16)

    pair_loop(q.shape[0] // rows_q, pair)


def norm_back_rows(values, gain_row, grad, base, out, total):
    total[...] = jnp.zeros_like(total)

    def chunk(k, _):
        rows = pl.ds(pl.multiple_of(k * 64, 64), 64)
        v = values[rows, :].astype(f32)
        inverse = inverse_rms(v)
        scaled = v * inverse
        g = grad[rows, :]
        weighted = g * gain_row[...]
        centre = jnp.mean(weighted * scaled, axis=-1, keepdims=True)
        out[rows, :] = base[rows, :].astype(f32) + inverse * (weighted - scaled * centre)
        total[...] += jnp.sum(g * scaled, axis=0, keepdims=True)
        return 0

    lax.fori_loop(0, values.shape[0] // 64, chunk, 0)


BACK_INPUTS = (
    "result", "dy", "hd", "n3", "r2", "ac", "cq", "ck", "cv", "n2",
    "enc", "r1", "mixed", "q", "k", "v", "n1", "x", "bias", "pre",
)
BACK_ORDER = ("xo", "xk", "xv", "xq", "o", "q", "k", "v")
SCATTER_ORDER = ("xo", "xq", "xk", "xv", "o", "q", "k", "v")


def backward_kernel(pieces, depth, blocks, *refs):
    refs = list(refs)

    def pop(count):
        return [refs.pop(0) for _ in range(count)]

    whole, down, source, live, gains = pop(5)
    ins = dict(zip(BACK_INPUTS, pop(len(BACK_INPUTS))))
    out, out_deep, layer_out, grad_in, grad_enc, gain_sums, folded = pop(7)
    held = dict(zip(BACK_INPUTS[:-1], pop(len(BACK_INPUTS) - 1)))
    load_sems, slots, slot_sems, pre, pre_sems, out_sems = pop(6)
    dgu, acc, dr2, dr1, low, dmix, dq, dk, dv, dck, dcv = pop(11)
    spread, moved, wanted, deal_send, deal_recv = pop(5)
    place = Place(depth)
    scatter = Scatter(place, pieces, blocks, (out, out_deep), refs)
    units = held["hd"].shape[1]
    rows = held["dy"].shape[0]

    loads = {
        name: pltpu.make_async_copy(ins[name], held[name], load_sems.at[i])
        for i, name in enumerate(BACK_INPUTS[:-1])
    }
    for load in loads.values():
        load.start()

    def need(*names):
        for name in names:
            loads.pop(name).wait()

    tiles = [(1, start, min(1024, units - start)) for start in range(0, units, 1024)]
    tiles += [(0, 8 * D + k, min(1024, 2 * units - k)) for k in range(0, 2 * units, 1024)]
    tiles += [(0, D * LEFT.index(w), D) for w in BACK_ORDER]
    stream = Stream((whole, down), tiles, slots, slot_sems)

    def ahead(k):
        return [
            pltpu.make_async_copy(
                ins["pre"].at[:, columns(j * units + k * 256, 256)],
                pre.at[k % 2, j],
                pre_sems.at[k % 2, j],
            )
            for j in (0, 1)
        ]

    for load in ahead(0):
        load.start()
    place.greet()
    redeal = Redeal(place, held["result"], spread, moved, wanted, deal_send, deal_recv)
    need("result")
    redeal.begin()

    need("dy", "hd")
    dy = held["dy"]
    scatter.produce(held["hd"], dy, 0)
    scatter.produce(held["hd"], dy, 512)
    for start in range(0, units, 1024):
        tile = stream.take()

        def chunk(n, _):
            k = start // 256 + n

            @pl.when(k + 1 < units // 256)
            def _():
                for load in ahead(k + 1):
                    load.start()

            for load in ahead(k):
                load.wait()
            part = against(dy[...], tile[pl.ds(pl.multiple_of(n * 256, 256), 256), :])
            act, slope = gelu_parts(pre[k % 2, 0])
            dgu[:, columns(k * 256, 256)] = (part * pre[k % 2, 1] * slope).astype(bf16)
            dgu[:, columns(units + k * 256, 256)] = (part * act).astype(bf16)
            return 0

        lax.fori_loop(0, min(1024, units - start) // 256, chunk, 0)
    need("n3")
    for start in range(0, 2 * units, 1024):
        scatter.produce(held["n3"], dgu, start)
        back_into(acc, dgu, start, min(1024, 2 * units - start), stream.take(), start == 0)
        if start == 2048:
            redeal.middle(source)
    need("r2")
    norm_back_rows(held["r2"], gains.at[2], acc, dy, dr2, gain_sums.at[2])
    low[...] = dr2[...].astype(bf16)
    need("ac")
    scatter.produce(held["ac"], low, 0)
    back_rounded(dmix, low, stream.take())
    need("cq", "ck", "cv")
    attend_back_pairs(
        (held["cq"], held["ck"], held["cv"], dmix), (dq, dck, dcv), live, cross_scores, None
    )
    need("n2", "enc")
    scatter.produce(held["n2"], dq, 0)
    scatter.produce(held["enc"], dck, 0)
    scatter.produce(held["enc"], dcv, 0)
    back_into(acc, dck, 0, D, stream.take(), True)
    back_into(acc, dcv, 0, D, stream.take(), False)
    enc_out = pltpu.make_async_copy(acc, grad_enc, out_sems.at[0])
    enc_out.start()
    enc_out.wait()
    back_into(acc, dq, 0, D, stream.take(), True)
    need("r1")
    norm_back_rows(held["r1"], gains.at[1], acc, dr2, dr1, gain_sums.at[1])
    low[...] = dr1[...].astype(bf16)
    need("mixed")
    scatter.produce(held["mixed"], low, 0)
    back_rounded(dmix, low, stream.take())
    need("q", "k", "v", "bias")
    attend_back_pairs(
        (held["q"], held["k"], held["v"], dmix),
        (dq, dk, dv),
        held["bias"],
        self_scores,
        folded,
    )
    need("n1")
    for grad in (dq, dk, dv):
        scatter.produce(held["n1"], grad, 0)
    for index, grad in enumerate((dq, dk, dv)):
        back_into(acc, grad, 0, D, stream.take(), index == 0)
    need("x")
    norm_back_rows(held["x"], gains.at[0], acc, dr1, dr2, gain_sums.at[0])
    in_out = pltpu.make_async_copy(dr2, grad_in, out_sems.at[1])
    in_out.start()
    redeal.end()
    deal_out = pltpu.make_async_copy(wanted, layer_out, out_sems.at[2])
    deal_out.start()
    scatter.close()
    in_out.wait()
    deal_out.wait()


def backward_all(whole, down, source, live, gains, acts, depth):
    tall, width = whole.shape
    tall_deep = down.shape[0]
    blocks = (tall // (4 * depth), tall_deep // (4 * depth))
    micro, length = acts["result"].shape[:2]
    rows, keys = micro * length, acts["enc"].shape[0]
    units, count = tall_deep, 8 * depth
    pieces = [(1, 0, 512), (1, 512, 512)]
    pieces += [(0, 8 * D + k, min(1024, 2 * units - k)) for k in range(0, 2 * units, 1024)]
    pieces += [(0, D * LEFT.index(w), D) for w in SCATTER_ORDER]
    anywhere = pl.BlockSpec(memory_space=pl.ANY)
    inside = pl.BlockSpec(memory_space=pltpu.VMEM)
    arrays = [acts[name] for name in BACK_INPUTS]
    spots = (micro, length // 8, D // depth)
    held = [pltpu.VMEM(a.shape, a.dtype) for a in arrays[:-1]]
    square = [pltpu.VMEM((rows, D), f32)] * 2 + [pltpu.VMEM((rows, D), bf16)] * 5
    return pl.pallas_call(
        functools.partial(backward_kernel, pieces, depth, blocks),
        out_shape=(
            jax.ShapeDtypeStruct((width // 128 * (blocks[0] // 2), 128), f32),
            jax.ShapeDtypeStruct((D // 128 * (blocks[1] // 2), 128), f32),
            jax.ShapeDtypeStruct((micro, length, D), bf16),
            jax.ShapeDtypeStruct((rows, D), f32),
            jax.ShapeDtypeStruct((keys, D), f32),
            jax.ShapeDtypeStruct((3, 1, D), f32),
            jax.ShapeDtypeStruct((micro * H, 1, length), f32),
        ),
        in_specs=[anywhere] * 2
        + [pl.BlockSpec(memory_space=pltpu.SMEM)]
        + [inside] * 2
        + [anywhere] * len(arrays),
        out_specs=(anywhere,) * 5 + (inside,) * 2,
        scratch_shapes=held
        + [
            pltpu.SemaphoreType.DMA((len(held),)),
            pltpu.VMEM((3, D, 1024), bf16),
            pltpu.SemaphoreType.DMA((3,)),
            pltpu.VMEM((2, 2, rows, 256), f32),
            pltpu.SemaphoreType.DMA((2, 2)),
            pltpu.SemaphoreType.DMA((3,)),
            pltpu.VMEM((rows, 2 * units), bf16),
            pltpu.VMEM((keys, D), f32),
        ]
        + square
        + [pltpu.VMEM((keys, D), bf16)] * 2
        + [
            pltpu.VMEM((count,) + spots, bf16),
            pltpu.VMEM((count,) + spots, bf16),
            pltpu.VMEM((micro, length, D), bf16),
            pltpu.SemaphoreType.DMA((2 * (count - 1),)),
            pltpu.SemaphoreType.DMA((2 * (count - 1),)),
        ]
        + Scatter.scratch(pieces, depth, blocks),
        compiler_params=pltpu.CompilerParams(
            collective_id=1, has_side_effects=True, vmem_limit_bytes=67043328
        ),
        name="backward",
    )(whole, down, source, live, gains, *arrays)


ACTS = ("hd", "n3", "r2", "ac", "cq", "ck", "cv", "n2", "r1", "mixed", "q", "k", "v", "n1", "bias")
LEFT = ("xk", "xv", "q", "k", "v", "o", "xq", "xo")


def norm_rows(values, gain_row, out):
    def chunk(k, _):
        rows = pl.ds(pl.multiple_of(k * 64, 64), 64)
        v = values[rows, :].astype(f32)
        out[rows, :] = (v * inverse_rms(v) * gain_row[...]).astype(bf16)
        return 0

    lax.fori_loop(0, values.shape[0] // 64, chunk, 0)


def by_columns(left, tile, width, put):
    def chunk(k, _):
        part = tile[:, :, :, :, columns(k * 256, 256)].reshape(-1, 256)
        put(k, jnp.dot(left[...], part, preferred_element_type=f32))
        return 0

    lax.fori_loop(0, width // 256, chunk, 0)


def attend_pairs(refs, out, marks, mask):
    q, k, v = refs
    rows_q = 128
    tall = k.shape[0] // (q.shape[0] // rows_q)
    even = lax.broadcasted_iota(jnp.int32, (1, 128), 1) < DH

    def pair(block, p):
        rows = pl.ds(pl.multiple_of(block * rows_q, rows_q), rows_q)
        keys = pl.ds(pl.multiple_of(block * tall, tall), tall)
        cols = columns(p * 128, 128)
        q2, k2, v2 = q[rows, cols], k[keys, cols], v[keys, cols]
        total = None
        for e in (0, 1):
            keep = even if e == 0 else jnp.logical_not(even)

            def half(value):
                return jnp.where(keep, value.astype(f32), 0.0).astype(bf16)

            probs = softmax_rows(mask(marks, against(half(q2), k2), block, 2 * p + e))
            term = jnp.dot(probs.astype(bf16), half(v2), preferred_element_type=f32)
            total = term if total is None else total + term
        out[rows, cols] = total.astype(bf16)

    pair_loop(q.shape[0] // rows_q, pair)


def gain_rows(table, gains, count):
    each = D // count
    values = jnp.sum(table[...], axis=1).astype(bf16)
    lane = lax.broadcasted_iota(jnp.int32, (128, D), 0)
    col = lax.broadcasted_iota(jnp.int32, (128, D), 1)
    device = lax.broadcasted_iota(jnp.int32, (count, D), 0)
    owner = lax.broadcasted_iota(jnp.int32, (count, D), 1) // each
    for k in range(3):
        pick = jnp.where(lane == k * each + col % each, 1.0, 0.0).astype(bf16)
        spread = jnp.dot(values, pick, preferred_element_type=f32)
        gains[k] = jnp.sum(jnp.where(device == owner, spread, 0.0), axis=0, keepdims=True)


def bias_blocks(table, buckets, allowed, by_offset, bias, count):
    first, share = 3 * (D // count), H * NB // count
    split = NB // share
    values = jnp.sum(table[...], axis=1).astype(bf16)
    lane = lax.broadcasted_iota(jnp.int32, (128, 128), 0) - first
    for block in range(bias.shape[0]):
        for part in range(split):
            hit = (lane + part * share == buckets[block, 0:1, :]) & (lane >= 0) & (lane < share)
            pick = jnp.where(hit, 1.0, 0.0).astype(bf16)
            found = jnp.dot(values, pick, preferred_element_type=f32)
            for device in range(count):
                by_offset[part, device] = found[device : device + 1]

        def head_bias(head, _):
            row = by_offset[0, head * split]
            for part in range(1, split):
                row = row + by_offset[part, head * split + part]
            grid = pltpu.roll(
                jnp.broadcast_to(row, (128, 128)), 0, 1, stride=1, stride_axis=0
            )
            bias[block, head] = jnp.where(allowed[block] > 0.0, grid, -1e30).astype(bf16)
            return 0

        lax.fori_loop(0, H, head_bias, 0)


def forward_kernel(pieces, depth, widths, *refs):
    refs = list(refs)

    def pop(count):
        return [refs.pop(0) for _ in range(count)]

    wide = pop(len(widths))
    (deep, tile, source, live, allowed, buckets, hidden, encoder, cotangent) = pop(9)
    whole, whole_deep, gains, dy, result, pre = pop(6)
    outs = dict(zip(ACTS, pop(len(ACTS))))
    staged, staged_deep, table, by_offset, x, enc, cot = pop(7)
    held = dict(zip(ACTS, pop(len(ACTS))))
    pre_held, result_held, slots, slot_sems, down_slot, spread, moved, wanted = pop(8)
    stage_sems, load_sems, out_sems, own_sems, send, recv, small_send, small_recv = pop(8)
    deal_send, deal_recv = pop(2)
    place = Place(depth)
    count = place.count
    rows, units = x.shape[0], held["hd"].shape[1]
    gather = Gather(
        place, pieces, (staged, staged_deep), (whole, whole_deep), own_sems, send, recv
    )
    staging, start = [], 0
    for i, width in enumerate(widths):
        target = staged.at[:, pl.ds(start, width)]
        staging.append(pltpu.make_async_copy(wide[i], target, stage_sems.at[i]))
        start += width
    staging.append(pltpu.make_async_copy(deep, staged_deep, stage_sems.at[len(widths)]))
    loads = [
        pltpu.make_async_copy(a, b, load_sems.at[i])
        for i, (a, b) in enumerate(((cotangent, cot), (hidden, x), (encoder, enc)))
    ]
    for copy in staging + loads:
        copy.start()
    place.greet()
    spread_small(place, tile, table, small_send, small_recv)
    for copy in staging:
        copy.wait()
    gather.open()
    redeal = Redeal(place, cot, spread, moved, wanted, deal_send, deal_recv)
    loads[0].wait()
    redeal.begin()
    collect_small(place, tile, table, small_send, small_recv)
    gain_rows(table, gains, count)
    loads[1].wait()
    loads[2].wait()
    norm_rows(x, gains.at[0], held["n1"])
    bias_blocks(table, buckets, allowed, by_offset, held["bias"], count)

    leaving = []

    def leave(name, source_ref=None, target=None):
        copy = pltpu.make_async_copy(
            held[name] if source_ref is None else source_ref,
            outs[name] if target is None else target,
            out_sems.at[len(leaving)],
        )
        copy.start()
        leaving.append(copy)

    leave("n1")
    leave("bias")

    tiles = [(D * k, D) for k in range(len(LEFT))]
    tiles += [(8 * D + k, min(1024, 2 * units - k)) for k in range(0, 2 * units, 1024)]

    def fetch(k):
        start, width = tiles[k]
        slot = k % slots.shape[0]
        return pltpu.make_async_copy(
            whole.at[:, :, :, :, pl.ds(start, width)],
            slots.at[slot, :, :, :, :, pl.ds(0, width)],
            slot_sems.at[slot],
        )

    def rounded(out):
        def put(k, part):
            out[:, columns(k * 256, 256)] = part.astype(bf16)

        return put

    def added(base, out):
        def put(k, part):
            cols = columns(k * 256, 256)
            out[:, cols] = base[:, cols].astype(f32) + part

        return put

    def units_of(k, tile_ref):
        start, width = tiles[k][0] - 8 * D, tiles[k][1]

        def put(n, part):
            at = start // 256 + n
            pre_held[:, columns(at * 256, 256)] = part

            @pl.when(at >= units // 256)
            def _():
                cols = columns((at - units // 256) * 256, 256)
                act, _ = gelu_parts(pre_held[:, cols])
                held["hd"][:, cols] = (act * part).astype(bf16)

        by_columns(held["n3"], tile_ref, width, put)

    def use(k):
        ref = slots.at[k % slots.shape[0]]
        name = LEFT[k] if k < len(LEFT) else ""
        if name in ("xk", "xv"):
            by_columns(enc, ref, D, rounded(held["c" + name[1]]))
            leave("c" + name[1])
        elif name in ("q", "k", "v"):
            by_columns(held["n1"], ref, D, rounded(held[name]))
            leave(name)
            if name == "v":
                attend_pairs(
                    (held["q"], held["k"], held["v"]),
                    held["mixed"],
                    held["bias"],
                    self_scores,
                )
                leave("mixed")
        elif name == "o":
            by_columns(held["mixed"], ref, D, added(x, held["r1"]))
            norm_rows(held["r1"], gains.at[1], held["n2"])
            leave("r1")
            leave("n2")
        elif name == "xq":
            by_columns(held["n2"], ref, D, rounded(held["cq"]))
            leave("cq")
            attend_pairs((held["cq"], held["ck"], held["cv"]), held["ac"], live, cross_scores)
            leave("ac")
        elif name == "xo":
            by_columns(held["ac"], ref, D, added(held["r1"], held["r2"]))
            norm_rows(held["r2"], gains.at[2], held["n3"])
            leave("r2")
            leave("n3")
        else:
            units_of(k, ref)

    done, fetched = 0, 0
    for t in range(len(pieces) + 3):
        gather.turn(t)
        if t < 3:
            continue
        kind, first, width = pieces[t - 3]
        if kind:
            copy = pltpu.make_async_copy(whole_deep, down_slot, slot_sems.at[0])
            copy.start()
            copy.wait()
            continue
        here = [k for k, (s, w) in enumerate(tiles) if first < s + w <= first + width]
        while fetched < len(tiles) and tiles[fetched][0] + tiles[fetched][1] <= first + width:
            if fetched >= done + slots.shape[0]:
                break
            fetch(fetched).start()
            fetched += 1
        for k in here:
            if k >= fetched:
                fetch(k).start()
                fetched += 1
            fetch(k).wait()
            use(k)
            done += 1
        if t == 4:
            redeal.middle(source)
    leave("", pre_held, pre)
    leave("hd")

    def last(k, part):
        cols = columns(k * 256, 256)
        result_held[:, cols] = (held["r2"][:, cols] + part).astype(bf16)

    by_columns(held["hd"], down_slot, D, last)
    leave("", result_held, result)
    redeal.end()
    leave("", wanted, dy)
    for copy in leaving:
        copy.wait()
    gather.close()


def forward_all(wide, deep, small, source, live, allowed, buckets, hidden, encoder, cotangent, depth):
    widths = [part.shape[1] for part in wide]
    width, tall = sum(widths), wide[0].shape[0]
    tall_deep, units = deep.shape[0], widths[-1]
    rows, keys = hidden.shape[0], encoder.shape[0]
    micro, length = cotangent.shape[:2]
    pieces = cut_columns([1024] + [2048] * 5)
    pieces.append((0, 11264, width - 11264))
    pieces.append((1, 0, D))
    copies = len(pieces) * (1 + 2 * (depth + 2))
    count = 8 * depth
    tile = jnp.zeros((8, 128), f32).at[0, : small.shape[0]].set(small.astype(f32))
    anywhere = pl.BlockSpec(memory_space=pl.ANY)
    inside = pl.BlockSpec(memory_space=pltpu.VMEM)
    spots = (micro, length // 8, D // depth)
    kinds = dict(
        hd=((rows, units), bf16),
        n3=((rows, D), bf16),
        r2=((rows, D), f32),
        ac=((rows, D), bf16),
        cq=((rows, D), bf16),
        ck=((keys, D), bf16),
        cv=((keys, D), bf16),
        n2=((rows, D), bf16),
        r1=((rows, D), f32),
        mixed=((rows, D), bf16),
        q=((rows, D), bf16),
        k=((rows, D), bf16),
        v=((rows, D), bf16),
        n1=((rows, D), bf16),
        bias=((micro, H, length, length), bf16),
    )
    results = pl.pallas_call(
        functools.partial(forward_kernel, pieces, depth, widths),
        out_shape=(
            jax.ShapeDtypeStruct((depth, 2, 2, 2 * tall, width), bf16),
            jax.ShapeDtypeStruct((depth, 2, 2, 2 * tall_deep, D), bf16),
            jax.ShapeDtypeStruct((3, 1, D), f32),
            jax.ShapeDtypeStruct((micro, length, D), bf16),
            jax.ShapeDtypeStruct((rows, D), bf16),
            jax.ShapeDtypeStruct((rows, 2 * units), f32),
        )
        + tuple(jax.ShapeDtypeStruct(*kinds[name]) for name in ACTS),
        in_specs=[anywhere] * (len(wide) + 1)
        + [inside, pl.BlockSpec(memory_space=pltpu.SMEM)]
        + [inside] * 3
        + [anywhere] * 3,
        out_specs=(anywhere,) * 2 + (inside,) + (anywhere,) * (3 + len(ACTS)),
        scratch_shapes=[
            pltpu.VMEM((tall, width), bf16),
            pltpu.VMEM((tall_deep, D), bf16),
            pltpu.VMEM((count, 8, 128), f32),
            pltpu.VMEM((2, count, 1, 128), f32),
            pltpu.VMEM((rows, D), bf16),
            pltpu.VMEM((keys, D), bf16),
            pltpu.VMEM((micro, length, D), bf16),
        ]
        + [pltpu.VMEM(*kinds[name]) for name in ACTS]
        + [
            pltpu.VMEM((rows, 2 * units), f32),
            pltpu.VMEM((rows, D), bf16),
            pltpu.VMEM((4, depth, 2, 2, 2 * tall, 1024), bf16),
            pltpu.SemaphoreType.DMA((4,)),
            pltpu.VMEM((depth, 2, 2, 2 * tall_deep, D), bf16),
            pltpu.VMEM((count,) + spots, bf16),
            pltpu.VMEM((count,) + spots, bf16),
            pltpu.VMEM((micro, length, D), bf16),
            pltpu.SemaphoreType.DMA((len(wide) + 1,)),
            pltpu.SemaphoreType.DMA((3,)),
            pltpu.SemaphoreType.DMA((len(ACTS) + 3,)),
            pltpu.SemaphoreType.DMA((len(pieces),)),
            pltpu.SemaphoreType.DMA((copies,)),
            pltpu.SemaphoreType.DMA((copies,)),
            pltpu.SemaphoreType.DMA((count - 1,)),
            pltpu.SemaphoreType.DMA((count - 1,)),
            pltpu.SemaphoreType.DMA((2 * (count - 1),)),
            pltpu.SemaphoreType.DMA((2 * (count - 1),)),
        ],
        compiler_params=pltpu.CompilerParams(
            collective_id=0, has_side_effects=True, vmem_limit_bytes=67043328
        ),
        name="forward",
    )(*wide, deep, tile, source, live, allowed, buckets, hidden, encoder, cotangent)
    whole, whole_deep, gains, dy, result, pre = results[:6]
    acts = dict(zip(ACTS, results[6:]))
    acts.update(
        dy=dy.reshape(rows, D),
        result=result.reshape(micro, length, D),
        pre=pre,
        x=hidden,
        enc=encoder,
    )
    return whole.reshape(-1, width), whole_deep.reshape(-1, D), gains, acts


def fused(
    depth,
    hidden,
    encoder,
    cotangent,
    segments,
    buckets,
    live,
    dealing,
    small,
    wide,
    feed_down,
):
    micro, _, length, _ = hidden.shape
    enc_count = encoder.shape[2]
    count = 8 * depth
    slots = jnp.arange(count, dtype=jnp.int32)
    inverse = jnp.sum(
        jnp.where(dealing[:, None, :] == slots[:, None], slots, 0), axis=2, dtype=jnp.int32
    )
    positions = jnp.arange(length, dtype=jnp.int32)
    allowed = (positions[None, :] <= positions[:, None])[None] & (
        segments[:, :, None] == segments[:, None, :]
    )
    turned = jnp.concatenate([buckets[:, :1], buckets[:, :0:-1]], axis=1)
    live_rows = jnp.arange(enc_count, dtype=jnp.int32)[None, None, :] < live[:, None, None]
    live_rows = jnp.broadcast_to(live_rows, (micro, 8, enc_count)).astype(f32)
    whole, down, gains, acts = forward_all(
        wide,
        feed_down,
        small,
        inverse,
        live_rows,
        allowed.astype(f32),
        jnp.broadcast_to(turned[:, None], (micro, 8, length)),
        hidden.reshape(micro * length, D),
        encoder.reshape(micro * enc_count, D),
        cotangent.reshape(micro, length, D),
        depth,
    )
    sums, piece_down, layer_out, grad_in, grad_enc, gain_sums, folded = backward_all(
        whole, down, dealing, live_rows, gains, acts, depth
    )
    offsets = folded.reshape(micro, H, length)[:, :, ::-1]
    onehot = (buckets[:, :, None] == jnp.arange(NB, dtype=jnp.int32)).astype(f32)
    g_bias = jnp.einsum("bho,boc->hc", offsets, onehot, precision=highest)
    small_grads = jnp.concatenate(
        [gain_sums[k, 0].reshape(count, -1) for k in range(3)] + [g_bias.reshape(count, -1)],
        axis=1,
    )
    small_sum = jnp.sum(
        lax.all_to_all(small_grads, AXIS, split_axis=0, concat_axis=0, tiled=True), axis=0
    )
    tall, tall_deep = wide[0].shape[0], feed_down.shape[0]
    sums = sums.reshape(-1, tall, 128)
    piece_down = piece_down.reshape(-1, tall_deep, 128)

    def unpack(tiles):
        return tiles.transpose(1, 0, 2).reshape(tiles.shape[1], -1)

    grads, start = [], 0
    for part in wide:
        tiles = part.shape[1] // 128
        grads.append(unpack(sums[start : start + tiles]))
        start += tiles
    part = D // count
    return (
        layer_out.reshape(hidden.shape),
        grad_in.reshape(hidden.shape),
        grad_enc.reshape(encoder.shape),
        small_sum[:part],
        small_sum[part : 2 * part],
        small_sum[2 * part : 3 * part],
        small_sum[3 * part :],
        *[grads[k] for k in (2, 3, 4, 5, 6, 0, 1, 7, 8, 9)],
        unpack(piece_down),
    )


def body(
    hidden,
    encoder,
    cotangent,
    segment_ids,
    rel_buckets,
    enc_rows,
    dealing,
    gain_self,
    gain_cross,
    gain_ffn,
    rel_bias,
    self_query,
    self_key,
    self_value,
    self_out,
    cross_query,
    cross_key,
    cross_value,
    cross_out,
    feed_gate,
    feed_up,
    feed_down,
):
    device = lax.axis_index(AXIS)
    micro, own, length, _ = hidden.shape
    enc_count = encoder.shape[2]
    blocks = micro * own
    first = device * own

    def mine(table):
        return lax.dynamic_slice_in_dim(table, first, own, axis=1).reshape(
            (blocks,) + table.shape[2:]
        )

    segments, buckets, live = mine(segment_ids), mine(rel_buckets), mine(enc_rows)
    small = jnp.concatenate([gain_self, gain_cross, gain_ffn, rel_bias])
    wide = (
        cross_key,
        cross_value,
        self_query,
        self_key,
        self_value,
        self_out,
        cross_query,
        cross_out,
        feed_gate,
        feed_up,
    )
    depth = kernel_depth(lax.axis_size(AXIS), self_query, feed_down) if own == 1 else 0
    if depth:
        return fused(
            depth,
            hidden,
            encoder,
            cotangent,
            segments,
            buckets,
            live,
            dealing,
            small,
            wide,
            feed_down,
        )
    grad_out = redeal(cotangent, jnp.argsort(dealing, axis=1)).reshape(blocks * length, D)

    smalls = lax.all_gather(small, AXIS, axis=0)
    part = gain_self.shape[0]
    gain_one, gain_two, gain_three = [
        smalls[:, k * part : (k + 1) * part].reshape(D).astype(f32) for k in range(3)
    ]
    bias_table = smalls[:, 3 * part :].reshape(H, NB).astype(f32)
    (wq, wk, wv, wo, xq, xk, xv, xo, gate, up), down = gather_weights(
        (
            self_query,
            self_key,
            self_value,
            self_out,
            cross_query,
            cross_key,
            cross_value,
            cross_out,
            feed_gate,
            feed_up,
        ),
        feed_down,
    )

    positions = jnp.arange(length, dtype=jnp.int32)
    allowed = (positions[None, :] <= positions[:, None])[None] & (
        segments[:, :, None] == segments[:, None, :]
    )
    cross_allowed = jnp.broadcast_to(
        jnp.arange(enc_count, dtype=jnp.int32)[None, None, :] < live[:, None, None],
        (blocks, length, enc_count),
    )
    onehot = (buckets[:, :, None] == jnp.arange(NB, dtype=jnp.int32)).astype(f32)
    per_offset = jnp.einsum("hc,boc->bho", bias_table, onehot, precision=highest)
    bias_grid = toeplitz_expand(per_offset.reshape(blocks * H, length)).reshape(
        blocks, H, length, length
    )

    wide_in = hidden.reshape(blocks * length, D).astype(f32)
    enc_in = encoder.reshape(blocks * enc_count, D)
    inv_one = inverse_rms(wide_in)
    normed_one = (wide_in * inv_one * gain_one).astype(bf16)
    queries = product(normed_one, wq).astype(bf16)
    keys_self = product(normed_one, wk).astype(bf16)
    values_self = product(normed_one, wv).astype(bf16)
    mixed_self, probs_self = attend(queries, keys_self, values_self, bias_grid, allowed)
    first_sum = wide_in + product(mixed_self, wo)
    inv_two = inverse_rms(first_sum)
    normed_two = (first_sum * inv_two * gain_two).astype(bf16)
    cross_queries = product(normed_two, xq).astype(bf16)
    cross_keys = product(enc_in, xk).astype(bf16)
    cross_values = product(enc_in, xv).astype(bf16)
    mixed_cross, probs_cross = attend(
        cross_queries, cross_keys, cross_values, None, cross_allowed
    )
    second_sum = first_sum + product(mixed_cross, xo)
    inv_three = inverse_rms(second_sum)
    normed_three = (second_sum * inv_three * gain_three).astype(bf16)
    gate_pre = product(normed_three, gate)
    up_pre = product(normed_three, up)
    act, slope = gelu_parts(gate_pre)
    hidden_units = (act * up_pre).astype(bf16)
    result = (second_sum + product(hidden_units, down)).astype(bf16)
    layer_out = redeal(result.reshape(micro, own, length, D), dealing)

    g_down = product_left(hidden_units, grad_out)
    grad_units = product_right(grad_out, down)
    grad_gate = (grad_units * up_pre * slope).astype(bf16)
    grad_up = (grad_units * act).astype(bf16)
    g_gate = product_left(normed_three, grad_gate)
    g_up = product_left(normed_three, grad_up)
    grad_three = product_right(grad_gate, gate) + product_right(grad_up, up)
    back, g_gain_three = norm_back(second_sum, inv_three, gain_three, grad_three)
    grad_second = grad_out.astype(f32) + back
    grad_low = grad_second.astype(bf16)
    g_xo = product_left(mixed_cross, grad_low)
    grad_mixed = product_right(grad_low, xo).astype(bf16)
    grad_cq, grad_ck, grad_cv, _ = attend_back(
        cross_queries, cross_keys, cross_values, probs_cross, grad_mixed
    )
    g_xq = product_left(normed_two, grad_cq)
    g_xk = product_left(enc_in, grad_ck)
    g_xv = product_left(enc_in, grad_cv)
    grad_enc = product_right(grad_ck, xk) + product_right(grad_cv, xv)
    back, g_gain_two = norm_back(first_sum, inv_two, gain_two, product_right(grad_cq, xq))
    grad_first = grad_second + back
    grad_low = grad_first.astype(bf16)
    g_so = product_left(mixed_self, grad_low)
    grad_mixed = product_right(grad_low, wo).astype(bf16)
    grad_sq, grad_sk, grad_sv, grad_scores = attend_back(
        queries, keys_self, values_self, probs_self, grad_mixed
    )
    offsets = toeplitz_fold(
        grad_scores.astype(f32).reshape(blocks * H, length, length)
    ).reshape(blocks, H, length)
    g_bias = jnp.einsum("bho,boc->hc", offsets, onehot, precision=highest).reshape(H * NB)
    g_sq = product_left(normed_one, grad_sq)
    g_sk = product_left(normed_one, grad_sk)
    g_sv = product_left(normed_one, grad_sv)
    grad_one = (
        product_right(grad_sq, wq) + product_right(grad_sk, wk) + product_right(grad_sv, wv)
    )
    back, g_gain_one = norm_back(wide_in, inv_one, gain_one, grad_one)
    grad_in = grad_first + back

    pieces, piece_down = scatter_grads(
        (g_sq, g_sk, g_sv, g_so, g_xq, g_xk, g_xv, g_xo, g_gate, g_up), g_down
    )
    count = smalls.shape[0]
    small_grads = jnp.concatenate(
        [g.reshape(count, -1) for g in (g_gain_one, g_gain_two, g_gain_three, g_bias)], axis=1
    )
    small_sum = jnp.sum(
        lax.all_to_all(small_grads, AXIS, split_axis=0, concat_axis=0, tiled=True), axis=0
    )
    return (
        layer_out,
        grad_in.reshape(hidden.shape),
        grad_enc.reshape(encoder.shape),
        small_sum[:part],
        small_sum[part : 2 * part],
        small_sum[2 * part : 3 * part],
        small_sum[3 * part :],
        *pieces,
        piece_down,
    )


def solution(mesh):
    block = P(None, AXIS, None, None)
    row = P(AXIS)
    matrix = P(AXIS, None)
    return jax.shard_map(
        body,
        mesh=mesh,
        in_specs=(block,) * 3 + (P(),) * 4 + (row,) * 4 + (matrix,) * 11,
        out_specs=(block,) * 3 + (row,) * 4 + (matrix,) * 11,
        check_vma=False,
    )
```

profile of v0, /device:TPU:0, one launch (start us, length us, event | category | flops | bytes accessed | tf_op | source)
XLA Modules:
  0.0 460.0 jit_solution(5911064952857347591)
XLA Ops:
  0.7 1.4 select_reduce_fusion.refs_12_
  2.0 0.9 dynamic-slice_reduce_fusion
  3.0 0.7 constant_dynamic-slice_fusion
  3.9 0.8 and_convert_fusion.refs_14_
  4.7 1.4 fusion.10.refs_11_
  7.3 214.2 %forward.1 = (bf16[4,2,2,64,13824]{4,3,2,1,0:T(8,128)(2,1)}, bf16[4,2,2,176,1024]{4,3,2,1,0:T(8,128)(2,1)}, f32[3,1,1024]{2,1,0:T(1,128)}, bf16[2,128,1024]{2,1,...) custom-call(bf16[32,1024]{1,0:T(8,128)(2,1)} %refs_0_.1, ...), custom_call_target="tpu_custom_call" | custom-call | tf_op jit(solution)/shard_map/forward/pallas_call | solution.py:1244
  221.5 214.8 %backward.1 = (f32[3456,128]{1,0:T(8,128)}, f32[704,128]{1,0:T(8,128)}, bf16[2,128,1024]{2,1,0:T(8,128)(2,1)}, f32[256,1024]{1,0:T(8,128)}, f32[512,1024]{1,0:T(...) custom-call(bf16[1024,13824]{1,0:T(8,128)(2,1)} %bitcast.103, bf16[2816,1024]{1,0:T(8,128)(2,1)} %bitcast.104, ...), custom_call_target="tpu_custom_call" | custom-call | tf_op jit(solution)/shard_map/backward/pallas_call | solution.py:901
  436.4 0.8 slice_reduce_fusion.2
  437.4 0.8 rev.7
  438.2 0.8 convolution_bitcast_fusion
  439.0 0.7 pad_maximum_fusion
  439.8 4.2 all-to-all-start
  443.9 1.4 fusion.15
  445.3 1.1 fusion.14
  446.5 0.8 copy.120
  447.2 0.7 copy.121
  447.9 0.7 copy.122
  448.8 0.8 copy.119
  449.8 0.8 copy.118
  450.6 0.7 copy.123
  451.3 0.7 copy.124
  455.8 1.9 copy.132
  457.7 1.0 copy.133
  458.7 1.3 copy.134
  (29 shorter events, 6.2 us)
Async XLA Ops:
  3.7 1.0 copy-start.3
  436.4 10.1 %copy-start.2 = (f32[704,128]{1,0:T(8,128)S(1)}, f32[704,128]{1,0:T(8,128)}, u32[]{:S(2)}) copy-start(f32[704,128]{1,0:T(8,128)} %get-tuple-element.85) | copy-start | bytes 1081348
  439.8 14.8 %all-to-all-start = ((f32[32,1,112]{2,1,0:T(1,128)}), f32[32,1,112]{2,1,0:T(1,128)S(1)}, u32[]{:S(2)}, u32[]{:S(2)}) async-start(f32[32,1,112]{2,1,0:T(1,128)} %bitcast.21), calls=%async_computation | async-start | bytes 32768 | tf_op jit(solution)/shard_map/all_to_all | solution.py:1358
  449.6 8.1 %copy-start.1 = (f32[256,1024]{1,0:T(8,128)S(1)}, f32[256,1024]{1,0:T(8,128)}, u32[]{:S(2)}) copy-start(f32[256,1024]{1,0:T(8,128)} %get-tuple-element.80) | copy-start | bytes 3145732
  451.9 6.7 %copy-start = (f32[512,1024]{1,0:T(8,128)S(1)}, f32[512,1024]{1,0:T(8,128)}, u32[]{:S(2)}) copy-start(f32[512,1024]{1,0:T(8,128)} %get-tuple-element.81) | copy-start | bytes 6291460
where the time goes:
time: 461 us; the launch traced here: 460 us
  Pallas kernels  429 us (93%)
  local copies, waits for them, and re-layouts  20.8 us (5%)
    pallas_call x1, Pallas kernels, backward_all(): pl.pallas_call(functools.partial(backward_kernel, pieces, depth, blocks),...  215 us
    pallas_call x1, Pallas kernels, forward_all(): pl.pallas_call(functools.partial(forward_kernel, pieces, depth, widths),...  214 us
  transfers between devices with their start and end apart: 1, of which 0 were waited for; matrix products, arithmetic and copies ran while one was open for 2% of the time, Pallas kernels for 0%

commit v1 on v0

--- a/solution.py
+++ b/solution.py
@@ -161,7 +161,10 @@
 
 MESH = pl.DeviceIdType.MESH
 RING = 3
-SLOTS = 5
+SLOTS = 7
+DRAIN = (1,) * 6
+GATHER_LAGS = (0, 2, 4, 5)
+SCATTER_LAGS = (0, 1, 2, 2, 1, 1)
 
 
 class Place:
@@ -298,7 +301,7 @@
 
     def turn(self, t):
         for stage in (3, 2, 1, 0):
-            self.advance(t - stage, stage)
+            self.advance(t - GATHER_LAGS[stage], stage)
 
     def close(self):
         for copy in self.sent:
@@ -315,7 +318,7 @@
             scratch[6:9],
         )
         self.steps = 1 + 2 * (place.depth + 2)
-        self.time = 0
+        self.done = [0] * 6
 
     @staticmethod
     def scratch(pieces, depth, blocks):
@@ -324,8 +327,8 @@
         return [
             pltpu.VMEM((SLOTS, 2, 2, depth, 2, 2, tall, 128), bf16),
             pltpu.VMEM((RING, 2, depth, 2, 2, tall, 128), bf16),
-            pltpu.VMEM((RING, 2, depth, 2, tall, 128), bf16),
-            pltpu.VMEM((RING, 2, depth, tall, 128), bf16),
+            pltpu.VMEM((RING + 1, 2, depth, 2, tall, 128), bf16),
+            pltpu.VMEM((RING + 1, 2, depth, tall, 128), bf16),
             pltpu.VMEM((RING, 2, depth - 1, tall, 128), bf16),
             pltpu.VMEM((RING, 2, 2, tall // 2, 128), f32),
             pltpu.SemaphoreType.DMA((2 * len(pieces),)),
@@ -348,7 +351,7 @@
         return self.cut(self.grads.at[(i % SLOTS, half) + quarter], i)
 
     def theirs(self, level, i, *index):
-        return self.cut(self.got[level].at[(i % RING,) + index], i)
+        return self.cut(self.got[level].at[(i % self.got[level].shape[0],) + index], i)
 
     def copy(self, source, target, i, step, device):
         return remote(source, target, self.send, self.recv, i * self.steps + step, device)
@@ -393,7 +396,7 @@
 
     def add(self, i, order, level, spots):
         rows = self.rows(i)
-        slot, ring, core = i % SLOTS, i % RING, self.place.core
+        slot, ring, core = i % SLOTS, i % self.got[level].shape[0], self.place.core
 
         def layer(z, _):
             for there, here in spots:
@@ -460,14 +463,18 @@
             self.rest(i, order).wait_send()
             self.keep(i, order).wait()
 
-    def turn(self):
+    def pump(self, lags=SCATTER_LAGS):
         for stage in (5, 4, 3, 2, 1):
-            self.advance(self.time - stage, stage)
-        self.time += 1
+            if self.done[stage] + lags[stage] <= self.done[stage - 1]:
+                self.advance(self.done[stage], stage)
+                self.done[stage] += 1
 
     def produce(self, left, right, column):
-        i = self.time
-        self.turn()
+        i = self.done[0]
+        self.pump()
+        while self.done[5] <= i - SLOTS:
+            self.pump()
+        self.done[0] += 1
         _, _, tiles, block = self.size(i)
         slot = i % SLOTS
         group = 1 if block % 32 == 0 else 2
@@ -494,8 +501,8 @@
         self.to_twin(i).start()
 
     def close(self):
-        while self.time < len(self.pieces) + 5:
-            self.turn()
+        while self.done[5] < len(self.pieces):
+            self.pump(DRAIN)
         for i in range(max(0, len(self.pieces) - RING), len(self.pieces)):
             self.settle(i)
 
@@ -667,12 +674,12 @@
     return jnp.where(live[block, 0:1, :] > 0.0, scores, masked_score)
 
 
-def pair_loop(count, body_of):
+def pair_loop(first, last, body_of):
     def one(index, _):
         body_of(index // (H // 2), index % (H // 2))
         return 0
 
-    lax.fori_loop(0, count * (H // 2), one, 0)
+    lax.fori_loop(first, last, one, 0)
 
 
 def softmax_rows(scores):
@@ -680,7 +687,7 @@
     return weights / jnp.sum(weights, axis=1, keepdims=True)
 
 
-def attend_back_pairs(refs, grads, marks, mask, folded):
+def attend_back_pairs(refs, grads, marks, mask, folded, first, last):
     q, k, v, da = refs
     dq, dk, dv = grads
     rows_q = 128
@@ -721,7 +728,7 @@
         dk[keys, cols] = sums[1].astype(bf16)
         dv[keys, cols] = sums[2].astype(bf16)
 
-    pair_loop(q.shape[0] // rows_q, pair)
+    pair_loop(first, last, pair)
 
 
 def norm_back_rows(values, gain_row, grad, base, out, total):
@@ -742,11 +749,48 @@
     lax.fori_loop(0, values.shape[0] // 64, chunk, 0)
 
 
+def small_tables(gain_sums, folded, buckets, tables, count):
+    each, share = D // count, H * NB // count
+    split, micro = NB // share, folded.shape[0] // H
+    lane = lax.broadcasted_iota(jnp.int32, (D, 128), 1)
+    col = lax.broadcasted_iota(jnp.int32, (D, 128), 0)
+    device = lax.broadcasted_iota(jnp.int32, (count, D), 0)
+    owner = lax.broadcasted_iota(jnp.int32, (count, D), 1) // each
+    total = jnp.zeros((count, 128), f32)
+    for k in range(3):
+        pick = jnp.where(lane == k * each + col % each, 1.0, 0.0)
+        mine = jnp.where(device == owner, gain_sums[k], 0.0)
+        total = total + jnp.dot(mine, pick, precision=highest, preferred_element_type=f32)
+    spot = lax.broadcasted_iota(jnp.int32, (128, 128), 1) - 3 * each
+    inside = (spot >= 0) & (spot < share)
+    for part in range(split):
+        found = jnp.zeros((H, 128), f32)
+        for block in range(micro):
+            hit = inside & (buckets[block] == spot + part * share)
+            rows = jnp.concatenate([folded[block * H + h] for h in range(H)], axis=0)
+            found = found + jnp.dot(
+                rows, jnp.where(hit, 1.0, 0.0), precision=highest, preferred_element_type=f32
+            )
+        for h in range(H):
+            j = h * split + part
+            row = total[j : j + 1] + found[h : h + 1]
+            tables[j] = jnp.broadcast_to(row, (8, 128))
+
+
+def swap_small(place, tables, got, send, recv, act):
+    def one(d, _):
+        peer = (place.me + d) % place.count
+        act(remote(tables.at[peer], got.at[place.me], send, recv, d - 1, peer))
+        return 0
+
+    lax.fori_loop(1, place.count, one, 0)
+
+
 BACK_INPUTS = (
     "result", "dy", "hd", "n3", "r2", "ac", "cq", "ck", "cv", "n2",
     "enc", "r1", "mixed", "q", "k", "v", "n1", "x", "bias", "pre",
 )
-BACK_ORDER = ("xo", "xk", "xv", "xq", "o", "q", "k", "v")
+BACK_ORDER = ("xo", "xq", "o", "xk", "xv", "q", "k", "v")
 SCATTER_ORDER = ("xo", "xq", "xk", "xv", "o", "q", "k", "v")
 
 
@@ -756,13 +800,14 @@
     def pop(count):
         return [refs.pop(0) for _ in range(count)]
 
-    whole, down, source, live, gains = pop(5)
+    whole, down, source, live, buckets, gains = pop(6)
     ins = dict(zip(BACK_INPUTS, pop(len(BACK_INPUTS))))
-    out, out_deep, layer_out, grad_in, grad_enc, gain_sums, folded = pop(7)
+    out, out_deep, layer_out, grad_in, grad_enc, small_out = pop(6)
     held = dict(zip(BACK_INPUTS[:-1], pop(len(BACK_INPUTS) - 1)))
     load_sems, slots, slot_sems, pre, pre_sems, out_sems = pop(6)
     dgu, acc, dr2, dr1, low, dmix, dq, dk, dv, dck, dcv = pop(11)
     spread, moved, wanted, deal_send, deal_recv = pop(5)
+    gain_sums, folded, tables, got, small_send, small_recv = pop(6)
     place = Place(depth)
     scatter = Scatter(place, pieces, blocks, (out, out_deep), refs)
     units = held["hd"].shape[1]
@@ -825,64 +870,108 @@
             return 0
 
         lax.fori_loop(0, min(1024, units - start) // 256, chunk, 0)
+        scatter.pump()
+    starts = list(range(0, 2 * units, 1024))
+    halves = rows // 128 * (H // 2)
+    quarter = halves // 4
+
+    def cross(part):
+        attend_back_pairs(
+            (held["cq"], held["ck"], held["cv"], dmix),
+            (dq, dck, dcv),
+            live,
+            cross_scores,
+            None,
+            part * quarter,
+            part * quarter + quarter,
+        )
+
+    def within(part):
+        attend_back_pairs(
+            (held["q"], held["k"], held["v"], dmix),
+            (dq, dk, dv),
+            held["bias"],
+            self_scores,
+            folded,
+            part * quarter,
+            part * quarter + quarter,
+        )
+
+    def feed():
+        start = starts.pop(0)
+        scatter.produce(held["n3"], dgu, start)
+
     need("n3")
-    for start in range(0, 2 * units, 1024):
-        scatter.produce(held["n3"], dgu, start)
-        back_into(acc, dgu, start, min(1024, 2 * units - start), stream.take(), start == 0)
-        if start == 2048:
-            redeal.middle(source)
+    feed()
+    for k, start in enumerate(range(0, 2 * units, 1024)):
+        back_into(acc, dgu, start, min(1024, 2 * units - start), stream.take(), k == 0)
+        if k == 2:
+            feed()
     need("r2")
     norm_back_rows(held["r2"], gains.at[2], acc, dy, dr2, gain_sums.at[2])
     low[...] = dr2[...].astype(bf16)
+    back_rounded(dmix, low, stream.take())
+    feed()
+    need("cq", "ck", "cv")
+    for part in range(4):
+        cross(part)
+        if starts:
+            feed()
+        else:
+            scatter.pump()
+    while starts:
+        feed()
+    redeal.middle(source)
     need("ac")
     scatter.produce(held["ac"], low, 0)
+    back_into(acc, dq, 0, D, stream.take(), True)
+    need("r1")
+    norm_back_rows(held["r1"], gains.at[1], acc, dr2, dr1, gain_sums.at[1])
+    low[...] = dr1[...].astype(bf16)
     back_rounded(dmix, low, stream.take())
-    need("cq", "ck", "cv")
-    attend_back_pairs(
-        (held["cq"], held["ck"], held["cv"], dmix), (dq, dck, dcv), live, cross_scores, None
-    )
     need("n2", "enc")
     scatter.produce(held["n2"], dq, 0)
+    need("q", "k", "v", "bias")
+    within(0)
+    within(1)
     scatter.produce(held["enc"], dck, 0)
+    within(2)
+    within(3)
     scatter.produce(held["enc"], dcv, 0)
     back_into(acc, dck, 0, D, stream.take(), True)
     back_into(acc, dcv, 0, D, stream.take(), False)
     enc_out = pltpu.make_async_copy(acc, grad_enc, out_sems.at[0])
     enc_out.start()
-    enc_out.wait()
-    back_into(acc, dq, 0, D, stream.take(), True)
-    need("r1")
-    norm_back_rows(held["r1"], gains.at[1], acc, dr2, dr1, gain_sums.at[1])
-    low[...] = dr1[...].astype(bf16)
     need("mixed")
     scatter.produce(held["mixed"], low, 0)
-    back_rounded(dmix, low, stream.take())
-    need("q", "k", "v", "bias")
-    attend_back_pairs(
-        (held["q"], held["k"], held["v"], dmix),
-        (dq, dk, dv),
-        held["bias"],
-        self_scores,
-        folded,
-    )
     need("n1")
     for grad in (dq, dk, dv):
         scatter.produce(held["n1"], grad, 0)
+    scatter.produce(held["n1"], dv, 512)
+    enc_out.wait()
     for index, grad in enumerate((dq, dk, dv)):
         back_into(acc, grad, 0, D, stream.take(), index == 0)
+        scatter.pump(DRAIN)
     need("x")
     norm_back_rows(held["x"], gains.at[0], acc, dr1, dr2, gain_sums.at[0])
     in_out = pltpu.make_async_copy(dr2, grad_in, out_sems.at[1])
     in_out.start()
+    scatter.pump(DRAIN)
+    small_tables(gain_sums, folded, buckets, tables, place.count)
+    swap_small(place, tables, got, small_send, small_recv, lambda copy: copy.start())
+    got[place.me] = tables[place.me]
+    scatter.pump(DRAIN)
     redeal.end()
     deal_out = pltpu.make_async_copy(wanted, layer_out, out_sems.at[2])
     deal_out.start()
     scatter.close()
+    swap_small(place, tables, got, small_send, small_recv, lambda copy: copy.wait())
+    small_out[...] = jnp.sum(got[...], axis=0)
     in_out.wait()
     deal_out.wait()
 
 
-def backward_all(whole, down, source, live, gains, acts, depth):
+def backward_all(whole, down, source, live, buckets, gains, acts, depth):
     tall, width = whole.shape
     tall_deep = down.shape[0]
     blocks = (tall // (4 * depth), tall_deep // (4 * depth))
@@ -891,7 +980,8 @@
     units, count = tall_deep, 8 * depth
     pieces = [(1, 0, 512), (1, 512, 512)]
     pieces += [(0, 8 * D + k, min(1024, 2 * units - k)) for k in range(0, 2 * units, 1024)]
-    pieces += [(0, D * LEFT.index(w), D) for w in SCATTER_ORDER]
+    pieces += [(0, D * LEFT.index(w), D) for w in SCATTER_ORDER[:-1]]
+    pieces += [(0, D * LEFT.index(SCATTER_ORDER[-1]) + k, 512) for k in (0, 512)]
     anywhere = pl.BlockSpec(memory_space=pl.ANY)
     inside = pl.BlockSpec(memory_space=pltpu.VMEM)
     arrays = [acts[name] for name in BACK_INPUTS]
@@ -906,19 +996,18 @@
             jax.ShapeDtypeStruct((micro, length, D), bf16),
             jax.ShapeDtypeStruct((rows, D), f32),
             jax.ShapeDtypeStruct((keys, D), f32),
-            jax.ShapeDtypeStruct((3, 1, D), f32),
-            jax.ShapeDtypeStruct((micro * H, 1, length), f32),
+            jax.ShapeDtypeStruct((8, 128), f32),
         ),
         in_specs=[anywhere] * 2
         + [pl.BlockSpec(memory_space=pltpu.SMEM)]
-        + [inside] * 2
+        + [inside] * 3
         + [anywhere] * len(arrays),
-        out_specs=(anywhere,) * 5 + (inside,) * 2,
+        out_specs=(anywhere,) * 5 + (inside,),
         scratch_shapes=held
         + [
             pltpu.SemaphoreType.DMA((len(held),)),
-            pltpu.VMEM((3, D, 1024), bf16),
-            pltpu.SemaphoreType.DMA((3,)),
+            pltpu.VMEM((2, D, 1024), bf16),
+            pltpu.SemaphoreType.DMA((2,)),
             pltpu.VMEM((2, 2, rows, 256), f32),
             pltpu.SemaphoreType.DMA((2, 2)),
             pltpu.SemaphoreType.DMA((3,)),
@@ -933,13 +1022,19 @@
             pltpu.VMEM((micro, length, D), bf16),
             pltpu.SemaphoreType.DMA((2 * (count - 1),)),
             pltpu.SemaphoreType.DMA((2 * (count - 1),)),
+            pltpu.VMEM((3, 1, D), f32),
+            pltpu.VMEM((micro * H, 1, length), f32),
+            pltpu.VMEM((count, 8, 128), f32),
+            pltpu.VMEM((count, 8, 128), f32),
+            pltpu.SemaphoreType.DMA((count - 1,)),
+            pltpu.SemaphoreType.DMA((count - 1,)),
         ]
         + Scatter.scratch(pieces, depth, blocks),
         compiler_params=pltpu.CompilerParams(
             collective_id=1, has_side_effects=True, vmem_limit_bytes=67043328
         ),
         name="backward",
-    )(whole, down, source, live, gains, *arrays)
+    )(whole, down, source, live, buckets, gains, *arrays)
 
 
 ACTS = ("hd", "n3", "r2", "ac", "cq", "ck", "cv", "n2", "r1", "mixed", "q", "k", "v", "n1", "bias")
@@ -965,7 +1060,7 @@
     lax.fori_loop(0, width // 256, chunk, 0)
 
 
-def attend_pairs(refs, out, marks, mask):
+def attend_pairs(refs, out, marks, mask, first, last):
     q, k, v = refs
     rows_q = 128
     tall = k.shape[0] // (q.shape[0] // rows_q)
@@ -988,7 +1083,7 @@
             total = term if total is None else total + term
         out[rows, cols] = total.astype(bf16)
 
-    pair_loop(q.shape[0] // rows_q, pair)
+    pair_loop(first, last, pair)
 
 
 def gain_rows(table, gains, count):
@@ -1004,30 +1099,29 @@
         gains[k] = jnp.sum(jnp.where(device == owner, spread, 0.0), axis=0, keepdims=True)
 
 
-def bias_blocks(table, buckets, allowed, by_offset, bias, count):
+def bias_block(table, buckets, allowed, by_offset, bias, count, block):
     first, share = 3 * (D // count), H * NB // count
     split = NB // share
     values = jnp.sum(table[...], axis=1).astype(bf16)
     lane = lax.broadcasted_iota(jnp.int32, (128, 128), 0) - first
-    for block in range(bias.shape[0]):
-        for part in range(split):
-            hit = (lane + part * share == buckets[block, 0:1, :]) & (lane >= 0) & (lane < share)
-            pick = jnp.where(hit, 1.0, 0.0).astype(bf16)
-            found = jnp.dot(values, pick, preferred_element_type=f32)
-            for device in range(count):
-                by_offset[part, device] = found[device : device + 1]
-
-        def head_bias(head, _):
-            row = by_offset[0, head * split]
-            for part in range(1, split):
-                row = row + by_offset[part, head * split + part]
-            grid = pltpu.roll(
-                jnp.broadcast_to(row, (128, 128)), 0, 1, stride=1, stride_axis=0
-            )
-            bias[block, head] = jnp.where(allowed[block] > 0.0, grid, -1e30).astype(bf16)
-            return 0
-
-        lax.fori_loop(0, H, head_bias, 0)
+    for part in range(split):
+        hit = (lane + part * share == buckets[block, 0:1, :]) & (lane >= 0) & (lane < share)
+        pick = jnp.where(hit, 1.0, 0.0).astype(bf16)
+        found = jnp.dot(values, pick, preferred_element_type=f32)
+        for device in range(count):
+            by_offset[part, device] = found[device : device + 1]
+
+    def head_bias(head, _):
+        row = by_offset[0, head * split]
+        for part in range(1, split):
+            row = row + by_offset[part, head * split + part]
+        grid = pltpu.roll(
+            jnp.broadcast_to(row, (128, 128)), 0, 1, stride=1, stride_axis=0
+        )
+        bias[block, head] = jnp.where(allowed[block] > 0.0, grid, -1e30).astype(bf16)
+        return 0
+
+    lax.fori_loop(0, H, head_bias, 0)
 
 
 def forward_kernel(pieces, depth, widths, *refs):
@@ -1042,7 +1136,7 @@
     outs = dict(zip(ACTS, pop(len(ACTS))))
     staged, staged_deep, table, by_offset, x, enc, cot = pop(7)
     held = dict(zip(ACTS, pop(len(ACTS))))
-    pre_held, result_held, slots, slot_sems, down_slot, spread, moved, wanted = pop(8)
+    pre_held, result_held, slots, slot_sems, down_sems, down_slot, spread, moved, wanted = pop(9)
     stage_sems, load_sems, out_sems, own_sems, send, recv, small_send, small_recv = pop(8)
     deal_send, deal_recv = pop(2)
     place = Place(depth)
@@ -1065,18 +1159,15 @@
         copy.start()
     place.greet()
     spread_small(place, tile, table, small_send, small_recv)
+    redeal = Redeal(place, cot, spread, moved, wanted, deal_send, deal_recv)
+    loads[0].wait()
+    redeal.begin()
     for copy in staging:
         copy.wait()
     gather.open()
-    redeal = Redeal(place, cot, spread, moved, wanted, deal_send, deal_recv)
-    loads[0].wait()
-    redeal.begin()
     collect_small(place, tile, table, small_send, small_recv)
-    gain_rows(table, gains, count)
     loads[1].wait()
     loads[2].wait()
-    norm_rows(x, gains.at[0], held["n1"])
-    bias_blocks(table, buckets, allowed, by_offset, held["bias"], count)
 
     leaving = []
 
@@ -1089,9 +1180,6 @@
         copy.start()
         leaving.append(copy)
 
-    leave("n1")
-    leave("bias")
-
     tiles = [(D * k, D) for k in range(len(LEFT))]
     tiles += [(8 * D + k, min(1024, 2 * units - k)) for k in range(0, 2 * units, 1024)]
 
@@ -1132,74 +1220,135 @@
 
         by_columns(held["n3"], tile_ref, width, put)
 
-    def use(k):
-        ref = slots.at[k % slots.shape[0]]
-        name = LEFT[k] if k < len(LEFT) else ""
-        if name in ("xk", "xv"):
-            by_columns(enc, ref, D, rounded(held["c" + name[1]]))
-            leave("c" + name[1])
-        elif name in ("q", "k", "v"):
-            by_columns(held["n1"], ref, D, rounded(held[name]))
+    whole_pairs = rows // 128 * (H // 2)
+    work = []
+
+    def piece_of(k):
+        kind, end = (1, 0) if k is None else (0, sum(tiles[k]))
+        ends = [s + w if kd == 0 else 0 for kd, s, w in pieces]
+        return next(i for i, e in enumerate(ends) if e >= end)
+
+    def with_tile(k, cost, act):
+        def run():
+            if k not in fetched:
+                fetch(k).start()
+                fetched.append(k)
+            fetch(k).wait()
+            act(slots.at[k % slots.shape[0]])
+            used.append(k)
+
+        work.append((piece_of(k), cost, run))
+
+    def then(cost, act):
+        work.append((0, cost, act))
+
+    fetched, used = [], []
+
+    def encoded(name):
+        def act(ref):
+            by_columns(enc, ref, D, rounded(held[name]))
             leave(name)
-            if name == "v":
+
+        return act
+
+    def projected(name, left):
+        def act(ref):
+            by_columns(held[left], ref, D, rounded(held[name]))
+            leave(name)
+
+        return act
+
+    def summed(left, base, total, gain, normed):
+        def act(ref):
+            by_columns(held[left], ref, D, added(base, held[total]))
+            norm_rows(held[total], gains.at[gain], held[normed])
+            leave(total)
+            leave(normed)
+
+        return act
+
+    def attention(cost, names, out, marks, mask):
+        for part in range(4):
+
+            def act(part=part):
                 attend_pairs(
-                    (held["q"], held["k"], held["v"]),
-                    held["mixed"],
-                    held["bias"],
-                    self_scores,
+                    [held[name] for name in names],
+                    held[out],
+                    marks,
+                    mask,
+                    part * whole_pairs // 4,
+                    (part + 1) * whole_pairs // 4,
                 )
-                leave("mixed")
-        elif name == "o":
-            by_columns(held["mixed"], ref, D, added(x, held["r1"]))
-            norm_rows(held["r1"], gains.at[1], held["n2"])
-            leave("r1")
-            leave("n2")
-        elif name == "xq":
-            by_columns(held["n2"], ref, D, rounded(held["cq"]))
-            leave("cq")
-            attend_pairs((held["cq"], held["ck"], held["cv"]), held["ac"], live, cross_scores)
-            leave("ac")
-        elif name == "xo":
-            by_columns(held["ac"], ref, D, added(held["r1"], held["r2"]))
-            norm_rows(held["r2"], gains.at[2], held["n3"])
-            leave("r2")
-            leave("n3")
-        else:
-            units_of(k, ref)
-
-    done, fetched = 0, 0
-    for t in range(len(pieces) + 3):
-        gather.turn(t)
-        if t < 3:
-            continue
-        kind, first, width = pieces[t - 3]
-        if kind:
-            copy = pltpu.make_async_copy(whole_deep, down_slot, slot_sems.at[0])
-            copy.start()
-            copy.wait()
-            continue
-        here = [k for k, (s, w) in enumerate(tiles) if first < s + w <= first + width]
-        while fetched < len(tiles) and tiles[fetched][0] + tiles[fetched][1] <= first + width:
-            if fetched >= done + slots.shape[0]:
-                break
-            fetch(fetched).start()
-            fetched += 1
-        for k in here:
-            if k >= fetched:
-                fetch(k).start()
-                fetched += 1
-            fetch(k).wait()
-            use(k)
-            done += 1
-        if t == 4:
-            redeal.middle(source)
-    leave("", pre_held, pre)
-    leave("hd")
+                if part == 3:
+                    leave(out)
+
+            then(cost, act)
+
+    def first_norm():
+        gain_rows(table, gains, count)
+        norm_rows(x, gains.at[0], held["n1"])
+        leave("n1")
+
+    work.append((-count, 3, first_norm))
+    for block in range(held["bias"].shape[0]):
+
+        def biases(block=block):
+            bias_block(table, buckets, allowed, by_offset, held["bias"], count, block)
+            if block == held["bias"].shape[0] - 1:
+                leave("bias")
+
+        work.append((-count, 3, biases))
+    for k, name in enumerate(("ck", "cv")):
+        with_tile(k, 4, encoded(name))
+    for k, name in enumerate(("q", "k", "v")):
+        with_tile(2 + k, 2, projected(name, "n1"))
+    attention(2, ("q", "k", "v"), "mixed", held["bias"], self_scores)
+    with_tile(5, 3, summed("mixed", x, "r1", 1, "n2"))
+    with_tile(6, 2, projected("cq", "n2"))
+    attention(3, ("cq", "ck", "cv"), "ac", live, cross_scores)
+    with_tile(7, 3, summed("ac", held["r1"], "r2", 2, "n3"))
+    for k in range(len(LEFT), len(tiles)):
+        with_tile(k, 3, functools.partial(units_of, k))
+
+    deep_pieces = [i for i, piece in enumerate(pieces) if piece[0]]
+    downs = []
+    for number, i in enumerate(deep_pieces):
+        cut = pl.ds(pieces[i][1], pieces[i][2])
+        downs.append(
+            pltpu.make_async_copy(
+                whole_deep.at[:, :, :, :, cut],
+                down_slot.at[:, :, :, :, cut],
+                down_sems.at[number],
+            )
+        )
 
     def last(k, part):
         cols = columns(k * 256, 256)
         result_held[:, cols] = (held["r2"][:, cols] + part).astype(bf16)
 
+    for t in range(len(pieces) + GATHER_LAGS[3]):
+        gather.turn(t)
+        ready = t - GATHER_LAGS[3]
+        if ready in deep_pieces:
+            downs[deep_pieces.index(ready)].start()
+        while len(fetched) < len(tiles) and piece_of(len(fetched)) <= ready:
+            if len(fetched) >= len(used) + slots.shape[0]:
+                break
+            fetch(len(fetched)).start()
+            fetched.append(len(fetched))
+        if t == 6:
+            redeal.middle(source)
+        spent = 0
+        while work and spent < 6 and work[0][0] <= ready:
+            _, cost, run = work.pop(0)
+            run()
+            spent += cost
+    while work:
+        work.pop(0)[2]()
+    leave("", pre_held, pre)
+    leave("hd")
+    for down in downs:
+        down.wait()
     by_columns(held["hd"], down_slot, D, last)
     leave("", result_held, result)
     redeal.end()
@@ -1215,9 +1364,9 @@
     tall_deep, units = deep.shape[0], widths[-1]
     rows, keys = hidden.shape[0], encoder.shape[0]
     micro, length = cotangent.shape[:2]
-    pieces = cut_columns([1024] + [2048] * 5)
-    pieces.append((0, 11264, width - 11264))
-    pieces.append((1, 0, D))
+    pieces = cut_columns([512, 512] + [1024] * 7)
+    pieces += [(0, k, min(1024, width - k)) for k in range(8 * D, width, 1024)]
+    pieces += [(1, 0, 512), (1, 512, 512)]
     copies = len(pieces) * (1 + 2 * (depth + 2))
     count = 8 * depth
     tile = jnp.zeros((8, 128), f32).at[0, : small.shape[0]].set(small.astype(f32))
@@ -1270,8 +1419,9 @@
         + [
             pltpu.VMEM((rows, 2 * units), f32),
             pltpu.VMEM((rows, D), bf16),
-            pltpu.VMEM((4, depth, 2, 2, 2 * tall, 1024), bf16),
-            pltpu.SemaphoreType.DMA((4,)),
+            pltpu.VMEM((5, depth, 2, 2, 2 * tall, 1024), bf16),
+            pltpu.SemaphoreType.DMA((5,)),
+            pltpu.SemaphoreType.DMA((2,)),
             pltpu.VMEM((depth, 2, 2, 2 * tall_deep, D), bf16),
             pltpu.VMEM((count,) + spots, bf16),
             pltpu.VMEM((count,) + spots, bf16),
@@ -1344,19 +1494,11 @@
         cotangent.reshape(micro, length, D),
         depth,
     )
-    sums, piece_down, layer_out, grad_in, grad_enc, gain_sums, folded = backward_all(
-        whole, down, dealing, live_rows, gains, acts, depth
-    )
-    offsets = folded.reshape(micro, H, length)[:, :, ::-1]
-    onehot = (buckets[:, :, None] == jnp.arange(NB, dtype=jnp.int32)).astype(f32)
-    g_bias = jnp.einsum("bho,boc->hc", offsets, onehot, precision=highest)
-    small_grads = jnp.concatenate(
-        [gain_sums[k, 0].reshape(count, -1) for k in range(3)] + [g_bias.reshape(count, -1)],
-        axis=1,
-    )
-    small_sum = jnp.sum(
-        lax.all_to_all(small_grads, AXIS, split_axis=0, concat_axis=0, tiled=True), axis=0
-    )
+    flipped = jnp.broadcast_to(buckets[:, ::-1, None], (micro, length, 128))
+    sums, piece_down, layer_out, grad_in, grad_enc, small_sum = backward_all(
+        whole, down, dealing, live_rows, flipped, gains, acts, depth
+    )
+    small_sum = small_sum[0]
     tall, tall_deep = wide[0].shape[0], feed_down.shape[0]
     sums = sums.reshape(-1, tall, 128)
     piece_down = piece_down.reshape(-1, tall_deep, 128)
@@ -1377,7 +1519,7 @@
         small_sum[:part],
         small_sum[part : 2 * part],
         small_sum[2 * part : 3 * part],
-        small_sum[3 * part :],
+        small_sum[3 * part : 3 * part + H * NB // count],
         *[grads[k] for k in (2, 3, 4, 5, 6, 0, 1, 7, 8, 9)],
         unpack(piece_down),
     )

time: 461 us -> 437 us (0.948)
  Pallas kernels: 429 us -> 411 us
    pallas_call x1, Pallas kernels: 214 us -> 203 us  [forward_all(): pl.pallas_call(functools.partial(forward_kernel, pieces, depth, widths),...]
    pallas_call x1, Pallas kernels: 215 us -> 209 us  [backward_all(): pl.pallas_call(functools.partial(backward_kernel, pieces, depth, blocks),...]
  transfers between devices with their start and end apart: 1 -> 0, of which waited for: 0 -> 0; matrix products, arithmetic and copies ran while one was open for 2% -> 0% of each run, Pallas kernels for 0% -> 0%
where the time goes in v1:
time: 437 us; the launch traced here: 436 us
  Pallas kernels  411 us (94%)
  local copies, waits for them, and re-layouts  20 us (5%)
    pallas_call x1, Pallas kernels, backward_all(): pl.pallas_call(functools.partial(backward_kernel, pieces, depth, blocks),...  209 us
    pallas_call x1, Pallas kernels, forward_all(): pl.pallas_call(functools.partial(forward_kernel, pieces, depth, widths),...  203 us

profile of v1, /device:TPU:0, one launch (start us, length us, event | category | flops | bytes accessed | tf_op | source)
XLA Modules:
  0.0 435.8 jit_solution(6104251521128849685)
XLA Ops:
  0.7 0.9 dynamic-slice_reduce_fusion
  1.5 1.4 select_reduce_fusion.refs_12_
  3.0 0.7 constant_dynamic-slice_fusion
  4.0 1.4 fusion.9.refs_11_
  6.6 0.8 and_convert_fusion.refs_14_
  7.4 0.8 broadcast_in_dim.18.refs_4_
  8.1 202.7 %forward.1 = (bf16[4,2,2,64,13824]{4,3,2,1,0:T(8,128)(2,1)}, bf16[4,2,2,176,1024]{4,3,2,1,0:T(8,128)(2,1)}, f32[3,1,1024]{2,1,0:T(1,128)}, bf16[2,128,1024]{2,1,...) custom-call(bf16[32,1024]{1,0:T(8,128)(2,1)} %refs_0_.1, ...), custom_call_target="tpu_custom_call" | custom-call | tf_op jit(solution)/shard_map/forward/pallas_call | solution.py:1393
  210.8 208.8 %backward.1 = (f32[3456,128]{1,0:T(8,128)}, f32[704,128]{1,0:T(8,128)}, bf16[2,128,1024]{2,1,0:T(8,128)(2,1)}, f32[256,1024]{1,0:T(8,128)}, f32[512,1024]{1,0:T(8,128)}, /*index=5*/f32[8,128]{1,0:T(8,128)}) custom-call(bf16[1024,13824]{1,0:T(8,128)(2,1)} %bitcast.106, bf16[2816,1024]{1,0:T(8,128)(2,1)} %bitcast.107, s32[2,32]{1,0:T(2,128)} %refs_2_.3, ...), custom_call_target="tpu_custom_call" | custom-call | tf_op jit(solution)/shard_map/backward/pallas_call | solution.py:991
  419.6 1.4 slice_bitcast_fusion
  421.0 1.4 slice_bitcast_fusion.1
  422.3 1.8 copy.106
  424.1 1.1 fusion.13
  425.3 0.7 copy.107
  426.0 0.7 copy.108
  426.9 0.8 copy.105
  427.9 0.8 copy.104
  428.7 0.7 copy.109
  429.4 0.7 copy.110
  430.0 0.7 copy.111
  430.7 0.7 copy.112
  432.0 0.7 copy.114
  432.7 0.8 copy.118
  433.5 1.0 copy.119
  434.5 1.3 copy.120
  (20 shorter events, 2.8 us)
Async XLA Ops:
  419.6 5.7 %copy-start.1 = (f32[3456,128]{1,0:T(8,128)S(1)}, f32[3456,128]{1,0:T(8,128)}, u32[]{:S(2)}) copy-start(f32[3456,128]{1,0:T(8,128)} %get-tuple-element.82) | copy-start | bytes 5308420
  426.9 5.8 %copy-start.3 = (bf16[2,128,1024]{2,1,0:T(8,128)(2,1)S(1)}, bf16[2,128,1024]{2,1,0:T(8,128)(2,1)}, u32[]{:S(2)}) copy-start(bf16[2,128,1024]{2,1,0:T(8,128)(2,1)} %get-tuple-element.78) | copy-start | bytes 1572868
  427.7 5.8 %copy-start.2 = (f32[256,1024]{1,0:T(8,128)S(1)}, f32[256,1024]{1,0:T(8,128)}, u32[]{:S(2)}) copy-start(f32[256,1024]{1,0:T(8,128)} %get-tuple-element.79) | copy-start | bytes 3145732
  430.0 4.4 %copy-start = (f32[512,1024]{1,0:T(8,128)S(1)}, f32[512,1024]{1,0:T(8,128)}, u32[]{:S(2)}) copy-start(f32[512,1024]{1,0:T(8,128)} %get-tuple-element.80) | copy-start | bytes 6291460

commit v2 on v1

--- a/solution.py
+++ b/solution.py
@@ -160,11 +160,17 @@
 
 
 MESH = pl.DeviceIdType.MESH
+
+
+def late_in_z(count):
+    return set(range(count - 5, count - 2))
+
+
 RING = 3
 SLOTS = 7
-DRAIN = (1,) * 6
+DRAIN = (1,) * 5
 GATHER_LAGS = (0, 2, 4, 5)
-SCATTER_LAGS = (0, 1, 2, 2, 1, 1)
+SCATTER_LAGS = (0, 1, 2, 2, 1)
 
 
 class Place:
@@ -216,6 +222,7 @@
         self.local, self.send, self.recv = local, send, recv
         self.steps = 1 + 2 * (place.depth + 2)
         self.sent = []
+        self.plane_first = late_in_z(len(pieces))
 
     def begin(self, copy):
         copy.start()
@@ -249,17 +256,22 @@
 
     def along_z(self, i, order, d):
         p = self.place
-        ref = self.wholes[self.pieces[i][0]].at[p.z, p.y, p.x, :, self.quarter(i, p.core, order)]
+        whole, cols = self.wholes[self.pieces[i][0]], self.quarter(i, p.core, order)
+        if i in self.plane_first:
+            ref = whole.at[p.z, :, :, :, cols]
+        else:
+            ref = whole.at[p.z, p.y, p.x, :, cols]
         return self.copy(ref, ref, i, 1 + order * (p.depth + 2) + d, p.over_z[d])
 
     def plane(self, i, order, second):
         p = self.place
         whole = self.wholes[self.pieces[i][0]]
         cols = self.quarter(i, p.core, order)
+        layers = p.z if i in self.plane_first else slice(None)
         if second:
-            ref = whole.at[:, :, p.x, :, cols] if order else whole.at[:, p.y, :, :, cols]
+            ref = whole.at[layers, :, p.x, :, cols] if order else whole.at[layers, p.y, :, :, cols]
         else:
-            ref = whole.at[:, p.y, p.x, :, cols]
+            ref = whole.at[layers, p.y, p.x, :, cols]
         device = p.over_x if order == second else p.over_y
         return self.copy(ref, ref, i, 1 + order * (p.depth + 2) + p.depth - 1 + second, device)
 
@@ -276,30 +288,55 @@
             self.own(i).start()
         for i in range(len(self.pieces)):
             self.own(i).wait()
+        for i in sorted(self.plane_first):
+            self.to_twin(i).wait_recv()
+            for order in (0, 1):
+                self.begin(self.plane(i, order, 0))
         for i in range(len(self.pieces)):
-            self.to_twin(i).wait_recv()
-            for d in range(self.place.depth - 1):
-                for order in (0, 1):
-                    self.begin(self.along_z(i, order, d))
+            if i not in self.plane_first:
+                self.to_twin(i).wait_recv()
+                self.all_z(i)
+
+    def all_z(self, i):
+        for d in range(self.place.depth - 1):
+            for order in (0, 1):
+                self.begin(self.along_z(i, order, d))
+
+    def early(self, t):
+        for i in sorted(self.plane_first):
+            for order in (0, 1):
+                if t == 1:
+                    self.plane(i, order, 0).wait_recv()
+                    self.begin(self.plane(i, order, 1))
+                elif t == 3:
+                    self.plane(i, order, 1).wait_recv()
+            if t == 3:
+                self.all_z(i)
 
     def advance(self, i, stage):
         if not 0 <= i < len(self.pieces):
             return
+        late = i in self.plane_first
         for order in (0, 1):
-            if stage == 0:
+            if late and stage < 2:
+                continue
+            if stage == 0 or late and stage == 2:
                 for d in range(self.place.depth - 1):
                     self.along_z(i, order, d).wait_recv()
+            if stage == 0:
                 self.begin(self.plane(i, order, 0))
             elif stage == 1:
                 self.plane(i, order, 0).wait_recv()
                 self.begin(self.plane(i, order, 1))
             elif stage == 2:
-                self.plane(i, order, 1).wait_recv()
+                if not late:
+                    self.plane(i, order, 1).wait_recv()
                 self.begin(self.across(i, order))
             else:
                 self.across(i, order).wait_recv()
 
     def turn(self, t):
+        self.early(t)
         for stage in (3, 2, 1, 0):
             self.advance(t - GATHER_LAGS[stage], stage)
 
@@ -318,7 +355,7 @@
             scratch[6:9],
         )
         self.steps = 1 + 2 * (place.depth + 2)
-        self.done = [0] * 6
+        self.done = [0] * 5
 
     @staticmethod
     def scratch(pieces, depth, blocks):
@@ -327,8 +364,8 @@
         return [
             pltpu.VMEM((SLOTS, 2, 2, depth, 2, 2, tall, 128), bf16),
             pltpu.VMEM((RING, 2, depth, 2, 2, tall, 128), bf16),
-            pltpu.VMEM((RING + 1, 2, depth, 2, tall, 128), bf16),
-            pltpu.VMEM((RING + 1, 2, depth, tall, 128), bf16),
+            pltpu.VMEM((2 * SCATTER_LAGS[2], 2, depth, 2, tall, 128), bf16),
+            pltpu.VMEM((2 * SCATTER_LAGS[3], 2, depth, tall, 128), bf16),
             pltpu.VMEM((RING, 2, depth - 1, tall, 128), bf16),
             pltpu.VMEM((RING, 2, 2, tall // 2, 128), f32),
             pltpu.SemaphoreType.DMA((2 * len(pieces),)),
@@ -449,22 +486,20 @@
                         ]
                 self.rest(i, order).start()
                 self.keep(i, order).start()
-        else:
             self.to_twin(i).wait_send()
             for order in (0, 1):
                 self.plane(i, order, 0).wait_send()
                 self.plane(i, order, 1).wait_send()
                 for d in range(p.depth - 1):
                     self.along_z(i, order, d).wait_send()
-                self.rest(i, order).wait_recv()
 
     def settle(self, i):
         for order in (0, 1):
-            self.rest(i, order).wait_send()
+            self.rest(i, order).wait()
             self.keep(i, order).wait()
 
     def pump(self, lags=SCATTER_LAGS):
-        for stage in (5, 4, 3, 2, 1):
+        for stage in (4, 3, 2, 1):
             if self.done[stage] + lags[stage] <= self.done[stage - 1]:
                 self.advance(self.done[stage], stage)
                 self.done[stage] += 1
@@ -472,7 +507,7 @@
     def produce(self, left, right, column):
         i = self.done[0]
         self.pump()
-        while self.done[5] <= i - SLOTS:
+        while self.done[4] <= i - SLOTS:
             self.pump()
         self.done[0] += 1
         _, _, tiles, block = self.size(i)
@@ -501,7 +536,7 @@
         self.to_twin(i).start()
 
     def close(self):
-        while self.done[5] < len(self.pieces):
+        while self.done[4] < len(self.pieces):
             self.pump(DRAIN)
         for i in range(max(0, len(self.pieces) - RING), len(self.pieces)):
             self.settle(i)

time: 437 us -> 425 us (0.973)
  Pallas kernels: 411 us -> 399 us
    pallas_call x1, Pallas kernels: 203 us -> 188 us  [forward_all(): pl.pallas_call(functools.partial(forward_kernel, pieces, depth, widths),...]
where the time goes in v2:
time: 425 us; the launch traced here: 423 us
  Pallas kernels  399 us (94%)
  local copies, waits for them, and re-layouts  20 us (5%)
    pallas_call x1, Pallas kernels, backward_all(): pl.pallas_call(functools.partial(backward_kernel, pieces, depth, blocks),...  211 us
    pallas_call x1, Pallas kernels, forward_all(): pl.pallas_call(functools.partial(forward_kernel, pieces, depth, widths),...  188 us

profile of v2, /device:TPU:0, one launch (start us, length us, event | category | flops | bytes accessed | tf_op | source)
XLA Modules:
  0.0 423.3 jit_solution(14787143438628893211)
XLA Ops:
  0.7 0.9 dynamic-slice_reduce_fusion
  1.5 1.4 select_reduce_fusion.refs_12_
  3.0 0.7 constant_dynamic-slice_fusion
  4.0 1.4 fusion.9.refs_11_
  6.6 0.8 and_convert_fusion.refs_14_
  7.4 0.8 broadcast_in_dim.18.refs_4_
  8.1 187.7 %forward.1 = (bf16[4,2,2,64,13824]{4,3,2,1,0:T(8,128)(2,1)}, bf16[4,2,2,176,1024]{4,3,2,1,0:T(8,128)(2,1)}, f32[3,1,1024]{2,1,0:T(1,128)}, bf16[2,128,1024]{2,1,...) custom-call(bf16[32,1024]{1,0:T(8,128)(2,1)} %refs_0_.1, ...), custom_call_target="tpu_custom_call" | custom-call | tf_op jit(solution)/shard_map/forward/pallas_call | solution.py:1428
  195.8 211.2 %backward.1 = (f32[3456,128]{1,0:T(8,128)}, f32[704,128]{1,0:T(8,128)}, bf16[2,128,1024]{2,1,0:T(8,128)(2,1)}, f32[256,1024]{1,0:T(8,128)}, f32[512,1024]{1,0:T(8,128)}, /*index=5*/f32[8,128]{1,0:T(8,128)}) custom-call(bf16[1024,13824]{1,0:T(8,128)(2,1)} %bitcast.106, bf16[2816,1024]{1,0:T(8,128)(2,1)} %bitcast.107, s32[2,32]{1,0:T(2,128)} %refs_2_.3, ...), custom_call_target="tpu_custom_call" | custom-call | tf_op jit(solution)/shard_map/backward/pallas_call | solution.py:1026
  407.1 1.4 slice_bitcast_fusion
  408.4 1.4 slice_bitcast_fusion.1
  409.8 1.8 copy.106
  411.6 1.1 fusion.13
  412.8 0.7 copy.107
  413.5 0.7 copy.108
  414.4 0.8 copy.105
  415.4 0.8 copy.104
  416.2 0.7 copy.109
  416.8 0.7 copy.110
  417.5 0.7 copy.111
  418.2 0.7 copy.112
  418.8 0.7 copy.113
  420.2 0.8 copy.118
  421.0 1.0 copy.119
  421.9 1.3 copy.120
  (20 shorter events, 2.8 us)
Async XLA Ops:
  407.1 5.7 %copy-start.1 = (f32[3456,128]{1,0:T(8,128)S(1)}, f32[3456,128]{1,0:T(8,128)}, u32[]{:S(2)}) copy-start(f32[3456,128]{1,0:T(8,128)} %get-tuple-element.82) | copy-start | bytes 5308420
  414.4 5.8 %copy-start.3 = (bf16[2,128,1024]{2,1,0:T(8,128)(2,1)S(1)}, bf16[2,128,1024]{2,1,0:T(8,128)(2,1)}, u32[]{:S(2)}) copy-start(bf16[2,128,1024]{2,1,0:T(8,128)(2,1)} %get-tuple-element.78) | copy-start | bytes 1572868
  415.2 5.8 %copy-start.2 = (f32[256,1024]{1,0:T(8,128)S(1)}, f32[256,1024]{1,0:T(8,128)}, u32[]{:S(2)}) copy-start(f32[256,1024]{1,0:T(8,128)} %get-tuple-element.79) | copy-start | bytes 3145732
  417.5 4.4 %copy-start = (f32[512,1024]{1,0:T(8,128)S(1)}, f32[512,1024]{1,0:T(8,128)}, u32[]{:S(2)}) copy-start(f32[512,1024]{1,0:T(8,128)} %get-tuple-element.80) | copy-start | bytes 6291460
